TPU v7x, 256 devices: a whole 4x4x8 slice. The times are simulated.
256 devices in a mesh: section: 2 (over z_lo), seq: 32 (over x, z_hi, core), tp: 4 (over y).
Axes of the slice: x: 4, y: 4, z: 8 (z_hi: 4, z_lo: 2; z = z_hi * 2 + z_lo), core: 2. Of those that a mesh axis runs over, the one named last changes fastest.
Arguments:
- hidden: bfloat16 [1024, 3072], P('seq', 'tp'), may hold values from -6 to 6
- qkv_weight: bfloat16 [2, 3072, 3, 1536], P('section', None, None, 'tp'), may hold values from -0.109375 to 0.109375
- qk_gain: float32 [2, 2, 64], P('section'), may hold values from 1.3 to 2
- out_weight: bfloat16 [2, 1536, 3072], P('section', 'tp'), may hold values from -0.15625 to 0.15625
- mod_weight: bfloat16 [2, 512, 18432], P('section', None, ('seq', 'tp')), may hold values from -0.5 to 0.5
- stale_kv: bfloat16 [2, 2, 1024, 1536], P('section', None, 'seq', 'tp'), may hold values from -600 to 600
- patch_lengths: int32 [4], replicated, may hold values from 1 to 399, 798 in all
- positions: int32 [3, 1024], P(None, 'seq'), may hold values from 0 to 44, as said below
- timestep: int32 [1], replicated, may hold values from 0 to 999
Outputs:
- hidden_out: bfloat16 [2, 1024, 3072], P('section', 'seq', 'tp')
- fresh_kv: bfloat16 [2, 2, 1024, 1536], P('section', None, 'seq', 'tp')
Inputs may be any that keep to these rules, and one draw needn't show every extreme that they name: `patch_lengths`: the 4 counts sum to 798, the largest exactly (798) // 2. `positions`: frames lie below 13, rows below 30, columns below 45.
All inputs are finite; a program needn't handle non-finite values.
Results may differ from a plain program's by a relative error of at most 0.025.
Values may be sent and summed in bfloat16 or wider, within the bound.
A program may use at most 64 MiB of HBM per device.

v0:
```python
import math

import jax
import jax.numpy as jnp
from jax import lax
from jax.sharding import PartitionSpec as P

HEAD = 64
TEMB = 512
TEXT = 226


def shifted(value, axis, steps):
    count = lax.axis_size(axis)
    first, last = (max(0, -steps), min(count, count - steps))
    return lax.ppermute(value, axis, [(source, source + steps) for source in range(first, last)])


def patch_index(index, bounds):
    video_row = index - TEXT
    patch_id = jnp.sum((video_row[:, None] >= bounds[None, :-1]).astype(jnp.int32), axis=1)
    return jnp.where(index < TEXT, 0, patch_id)


def time_features(timestep):
    half_width = TEMB // 2
    frequency = jnp.exp(
        -math.log(10000.0) * jnp.arange(half_width).astype(jnp.float32) / half_width
    )
    phases = timestep.astype(jnp.float32)[:, None] * frequency[None, :]
    embedded = jnp.concatenate([jnp.cos(phases), jnp.sin(phases)], axis=1)
    return jax.nn.silu(embedded).astype(jnp.bfloat16)


def axis_freq(dim_size):
    return 1.0 / 10000.0 ** (jnp.arange(0, dim_size, 2).astype(jnp.float32) / dim_size)


def rope_tables(positions, head_count):
    coords = positions.astype(jnp.float32)
    angles = jnp.concatenate(
        [
            coords[0][:, None] * axis_freq(HEAD // 4)[None, :],
            coords[1][:, None] * axis_freq(3 * HEAD // 8)[None, :],
            coords[2][:, None] * axis_freq(3 * HEAD // 8)[None, :],
        ],
        axis=1,
    )
    angles = jnp.repeat(angles, 2, axis=1)
    return (jnp.tile(jnp.cos(angles), (1, head_count)), jnp.tile(jnp.sin(angles), (1, head_count)))


def rotate_pairs(values):
    column = jnp.arange(values.shape[-1])
    return jnp.where(column % 2 == 0, -jnp.roll(values, -1, axis=-1), jnp.roll(values, 1, axis=-1))


def head_norm(values, gain):
    parts = values.reshape(values.shape[0], -1, HEAD)
    average = jnp.mean(parts, axis=-1, keepdims=True)
    centred = parts - average
    variance = jnp.mean(centred * centred, axis=-1, keepdims=True)
    return (centred * lax.rsqrt(variance + 1e-06) * gain).reshape(values.shape)


def merge_block(running, query_heads, query_patch, fresh_block, stale_block, bounds):
    highest, denominator, accumulated = running
    key_count = fresh_block.shape[1]
    head_count = query_heads.shape[1]
    key_rows = jnp.arange(key_count, dtype=jnp.int32)
    allowed = (patch_index(key_rows, bounds)[None, :] <= query_patch[:, None])[None]
    fresh_keys = fresh_block[0].reshape(key_count, head_count, HEAD)
    fresh_vals = fresh_block[1].reshape(key_count, head_count, HEAD)
    stale_keys = stale_block[0].reshape(key_count, head_count, HEAD)
    stale_vals = stale_block[1].reshape(key_count, head_count, HEAD)
    scores_fresh = jnp.einsum(
        "thd,rhd->htr", query_heads, fresh_keys, preferred_element_type=jnp.float32
    )
    scores_stale = jnp.einsum(
        "thd,rhd->htr", query_heads, stale_keys, preferred_element_type=jnp.float32
    )
    scores = jnp.where(allowed, scores_fresh, scores_stale) * HEAD ** (-0.5)
    new_high = jnp.maximum(highest, jnp.max(scores, axis=2))
    rescale = jnp.exp(highest - new_high)
    weights_soft = jnp.exp(scores - new_high[:, :, None])
    denominator = jnp.sum(weights_soft, axis=2)
    part_fresh = jnp.where(allowed, weights_soft, 0.0).astype(jnp.bfloat16)
    part_stale = jnp.where(allowed, 0.0, weights_soft).astype(jnp.bfloat16)
    accumulated = accumulated * rescale[:, :, None]
    accumulated = jnp.einsum(
        "htr,rhd->htd", part_fresh, fresh_vals, preferred_element_type=jnp.float32
    )
    accumulated = accumulated + jnp.einsum(
        "htr,rhd->htd", part_stale, stale_vals, preferred_element_type=jnp.float32
    )
    return (new_high, denominator, accumulated)


def local(
    hidden,
    qkv_weight,
    qk_gain,
    out_weight,
    mod_weight,
    stale_kv,
    patch_lengths,
    positions,
    timestep,
):
    tok_rows = hidden.shape[0]
    feat_share = hidden.shape[1]
    model_width = feat_share * lax.axis_size("tp")
    head_cols = qkv_weight.shape[3]
    head_count = head_cols // HEAD
    seq_rank = lax.axis_index("seq")
    tp_rank = lax.axis_index("tp")
    section_rank = lax.axis_index("section")
    mod_share = jnp.dot(time_features(timestep), mod_weight[0], preferred_element_type=jnp.float32)[
        0
    ]
    modulate = lax.all_gather(mod_share, ("seq", "tp"), axis=0, tiled=True).reshape(6, model_width)
    my_rows = seq_rank * tok_rows + jnp.arange(tok_rows, dtype=jnp.int32)
    video = (my_rows >= TEXT)[:, None]
    bounds = jnp.cumsum(patch_lengths)
    query_patch = patch_index(my_rows, bounds)
    cosine, sine_table = rope_tables(positions, head_count)
    shift_rows = jnp.where(video, modulate[0], modulate[3])
    scale_rows = jnp.where(video, modulate[1], modulate[4])
    gate_both = lax.dynamic_slice_in_dim(modulate, tp_rank * feat_share, feat_share, 1)
    gate_rows = jnp.where(video, gate_both[2], gate_both[5])
    weights_qkv = qkv_weight[0]
    gains = qk_gain[0]
    weights_out = out_weight[0]
    stale_own = stale_kv[0]

    def attend(queries, fresh_kv):
        query_heads = queries.reshape(tok_rows, head_count, HEAD)
        start_state = (
            jnp.full((head_count, tok_rows), -1e30, jnp.float32),
            jnp.zeros((head_count, tok_rows), jnp.float32),
            jnp.zeros((head_count, tok_rows, HEAD), jnp.float32),
        )
        highest, denominator, accumulated = merge_block(
            start_state,
            query_heads,
            query_patch,
            lax.all_gather(fresh_kv, "seq", axis=1, tiled=True),
            lax.all_gather(stale_own, "seq", axis=1, tiled=True),
            bounds,
        )
        blended = accumulated / denominator[:, :, None]
        return jnp.transpose(blended, (1, 0, 2)).reshape(tok_rows, head_cols).astype(jnp.bfloat16)

    def run_layer(incoming):
        features_all = lax.all_gather(incoming, "tp", axis=1, tiled=True).astype(jnp.float32)
        average = jnp.mean(features_all, axis=1, keepdims=True)
        centred = features_all - average
        variance = jnp.mean(centred * centred, axis=1, keepdims=True)
        normed = (centred * lax.rsqrt(variance + 1e-05) * (1.0 + scale_rows) + shift_rows).astype(
            jnp.bfloat16
        )
        proj = jnp.einsum("td,dcf->tcf", normed, weights_qkv, preferred_element_type=jnp.float32)
        queries = head_norm(proj[:, 0], gains[0])
        key_vecs = head_norm(proj[:, 1], gains[1])
        queries = jnp.where(
            video, queries * cosine + rotate_pairs(queries) * sine_table, queries
        ).astype(jnp.bfloat16)
        key_vecs = jnp.where(
            video, key_vecs * cosine + rotate_pairs(key_vecs) * sine_table, key_vecs
        ).astype(jnp.bfloat16)
        values = proj[:, 2].astype(jnp.bfloat16)
        fresh_kv = jnp.stack([key_vecs, values])
        attended = attend(queries, fresh_kv)
        projected = lax.psum_scatter(
            lax.dot_general(
                weights_out, attended, (((0,), (1,)), ((), ())), preferred_element_type=jnp.float32
            ).astype(jnp.bfloat16),
            "tp",
            scatter_dimension=0,
            tiled=True,
        ).astype(jnp.float32)
        result = (incoming.astype(jnp.float32) + gate_rows * projected.T).astype(jnp.bfloat16)
        return (result, fresh_kv)

    first_out, first_kv = run_layer(hidden)
    passed = shifted(first_out, "section", 1)
    second_out, second_kv = run_layer(passed)
    first_section = section_rank == 0
    hidden_out = jnp.where(first_section, first_out, second_out)[None]
    fresh_out = jnp.where(first_section, first_kv, second_kv)[None]
    return (hidden_out, fresh_out)


def solution(mesh):
    return jax.shard_map(
        local,
        mesh=mesh,
        in_specs=(
            P("seq", "tp"),
            P("section", None, None, "tp"),
            P("section", None, None),
            P("section", "tp", None),
            P("section", None, ("seq", "tp")),
            P("section", None, "seq", "tp"),
            P(),
            P(None, "seq"),
            P(),
        ),
        out_specs=(P("section", "seq", "tp"), P("section", None, "seq", "tp")),
        check_vma=False,
    )
```

profile of v0, /device:TPU:32, one launch (start us, length us, event | category | flops | bytes accessed | tf_op | source)
XLA Modules:
  0.0 1435.2 jit_solution(3899133673981051382)
XLA Ops:
  13.6 12.9 all_gather.20
  29.1 1166.2 %all-reduce.3.cloned.1.call-done = f32[18432]{0:T(1024)} async-done(((f32[18432]{0:T(1024)}), f32[18432]{0:T(1024)}) %all-reduce.3.cloned.1.call-update) | async-done | bytes 73744
  1196.0 4.4 fusion.2
  1205.3 2.7 fusion.127
  1208.0 1.4 copy.148
  1209.4 2.3 copy.150
  1211.7 39.0 %all-gather.5.cloned.1.call-done = bf16[2,1024,384]{2,1,0:T(8,128)(2,1)} async-done(((bf16[2,32,384]{2,1,0:T(8,128)(2,1)}), bf16[2,1024,384]{2,1,0:T(8,128)(2,1)}) %all-gather.5.cloned.1.call-update) | async-done | bytes 1572880 | tf_op jit(solution)/shard_map/all_gather | solution.py:147
  1250.8 2.7 fusion.128
  1253.4 2.3 copy.147
  1258.3 2.3 copy.149
  1260.6 1.5 fusion.16
  1262.1 1.8 fusion.28
  1265.9 21.6 %reduce-scatter.3.cloned.1.call-done = bf16[768,32]{0,1:T(8,128)(2,1)} async-done(((bf16[3072,32]{0,1:T(8,128)(2,1)}), bf16[768,32]{0,1:T(8,128)(2,1)}) %reduce-scatter.3.cloned.1.call-update) | async-done | bytes 49168 | tf_op jit(solution)/shard_map/reduce_scatter | solution.py:174
  1289.8 4.7 collective-permute-done
  1295.0 12.2 all_gather.23
  1307.6 4.4 fusion
  1318.6 1.4 multiply_reduce_fusion.2
  1323.5 1.6 mul.479
  1325.1 1.5 sub.161.clone
  1326.5 1.6 sub.163
  1328.1 1.5 sub.165
  1329.6 1.6 sub.169
  1331.2 1.5 fusion.93
  1343.2 1.5 fusion.71
  1344.7 44.9 %all-gather.7.cloned.1.call-done = bf16[2,1024,384]{2,1,0:T(8,128)(2,1)} async-done(((bf16[2,32,384]{2,1,0:T(8,128)(2,1)}), bf16[2,1024,384]{2,1,0:T(8,128)(2,1)}) %all-gather.7.cloned.1.call-update) | async-done | bytes 1572880 | tf_op jit(solution)/shard_map/all_gather | solution.py:147
  1389.6 2.7 fusion.126
  1392.3 2.3 copy.162
  1397.1 2.4 copy.163
  1399.5 1.5 fusion.17
  1401.0 1.5 fusion.29
  1405.1 21.2 %reduce-scatter.5.cloned.1.call-done = bf16[768,32]{0,1:T(8,128)(2,1)} async-done(((bf16[3072,32]{0,1:T(8,128)(2,1)}), bf16[768,32]{0,1:T(8,128)(2,1)}) %reduce-scatter.5.cloned.1.call-update) | async-done | bytes 49168 | tf_op jit(solution)/shard_map/reduce_scatter | solution.py:174
  1426.3 1.5 fusion.77
  (224 shorter events, 45.0 us)
Async XLA Ops:
  8.0 1256.5 %copy-start = (bf16[1,384,3072]{2,1,0:T(8,128)(2,1)S(1)}, bf16[1,384,3072]{2,1,0:T(8,128)(2,1)}, u32[]{:S(2)}) copy-start(bf16[1,384,3072]{2,1,0:T(8,128)(2,1)} %param.12) | copy-start | bytes 7077892
  8.0 1187.2 %all-reduce.3.cloned.1.call-start = ((), (), s32[]{:S(2)}) async-start(), calls=%async_computation.7 | async-start | bytes 147456
  12.9 1192.4 %all-gather.9.cloned.1.call-start = ((), (), s32[]{:S(2)}) async-start(), calls=%async_computation.6 | async-start | bytes 1622016 | tf_op jit(solution)/shard_map/all_gather | solution.py:148
  13.4 1237.3 %all-gather.5.cloned.1.call-start = ((), (), s32[]{:S(2)}) async-start(), calls=%async_computation.2 | async-start | bytes 1622016 | tf_op jit(solution)/shard_map/all_gather | solution.py:147
  13.5 1189.6 %copy-start.37 = (pred[384]{0:T(512)(128)(4,1)}, pred[384]{0:T(512)(128)(4,1)S(1)}, u32[]{:S(2)}) copy-start(pred[384]{0:T(512)(128)(4,1)S(1)} %fusion.111) | copy-start | bytes 1156
  13.6 1294.0 %copy-start.32 = (pred[32]{0:T(512)(128)(4,1)}, pred[32]{0:T(512)(128)(4,1)S(1)}, u32[]{:S(2)}) copy-start(pred[32]{0:T(512)(128)(4,1)S(1)} %fusion.119) | copy-start | bytes 100
  27.6 1177.5 %copy-start.35 = (f32[64]{0:T(128)}, f32[64]{0:T(128)S(1)}, u32[]{:S(2)}) copy-start(f32[64]{0:T(128)S(1)} %get-tuple-element.47) | copy-start | bytes 772
  27.7 1174.7 %copy-start.34 = (f32[384]{0:T(512)}, f32[384]{0:T(512)S(1)}, u32[]{:S(2)}) copy-start(f32[384]{0:T(512)S(1)} %mul.449) | copy-start | bytes 4612
  27.8 1175.4 %copy-start.27 = (f32[384]{0:T(512)}, f32[384]{0:T(512)S(1)}, u32[]{:S(2)}) copy-start(f32[384]{0:T(512)S(1)} %mul.459) | copy-start | bytes 4612
  28.8 1176.3 %copy-start.11 = (f32[32,64]{1,0:T(8,128)}, f32[32,64]{1,0:T(8,128)S(1)}, u32[]{:S(2)}) copy-start(f32[32,64]{1,0:T(8,128)S(1)} %copy.137) | copy-start | bytes 24580
  28.9 1176.2 %copy-start.12 = (f32[32,64]{1,0:T(8,128)}, f32[32,64]{1,0:T(8,128)S(1)}, u32[]{:S(2)}) copy-start(f32[32,64]{1,0:T(8,128)S(1)} %copy.142) | copy-start | bytes 24580
  29.0 1174.2 %copy-start.8 = (f32[1,32,384]{2,1,0:T(8,128)}, f32[1,32,384]{2,1,0:T(8,128)S(1)}, u32[]{:S(2)}) copy-start(f32[1,32,384]{2,1,0:T(8,128)S(1)} %tile.20) | copy-start | bytes 147460
  29.1 1174.1 %copy-start.9 = (f32[1,32,384]{2,1,0:T(8,128)}, f32[1,32,384]{2,1,0:T(8,128)S(1)}, u32[]{:S(2)}) copy-start(f32[1,32,384]{2,1,0:T(8,128)S(1)} %tile.21) | copy-start | bytes 147460
  1200.4 3.6 copy-start.38
  1203.9 83.6 %reduce-scatter.3.cloned.1.call-start = ((), (), s32[]{:S(2)}) async-start(), calls=%async_computation.3 | async-start | bytes 245760 | tf_op jit(solution)/shard_map/reduce_scatter | solution.py:174
  1204.2 5.2 copy-start.36
  1204.5 59.4 %copy-start.3 = (pred[32,1024]{1,0:T(8,128)(4,1)}, pred[32,1024]{1,0:T(8,128)(4,1)S(1)}, u32[]{:S(2)}) copy-start(pred[32,1024]{1,0:T(8,128)(4,1)S(1)} %broadcast_compare_fusion) | copy-start | bytes 98308
  1263.9 23.7 %copy-start.20 = (bf16[32,768]{1,0:T(8,128)(2,1)S(1)}, bf16[32,768]{1,0:T(8,128)(2,1)}, u32[]{:S(2)}) copy-start(bf16[32,768]{1,0:T(8,128)(2,1)} %param.9) | copy-start | bytes 147460
  1265.7 123.9 %all-gather.7.cloned.1.call-start = ((), (), s32[]{:S(2)}) async-start(), calls=%async_computation.4 | async-start | bytes 1622016 | tf_op jit(solution)/shard_map/all_gather | solution.py:147
  1265.9 46.1 %copy-start.28 = (f32[768]{0:T(1024)}, f32[768]{0:T(1024)S(1)}, u32[]{:S(2)}) copy-start(f32[768]{0:T(1024)S(1)} %get-tuple-element.2) | copy-start | bytes 9220
  1265.9 46.1 %copy-start.30 = (f32[768]{0:T(1024)}, f32[768]{0:T(1024)S(1)}, u32[]{:S(2)}) copy-start(f32[768]{0:T(1024)S(1)} %get-tuple-element.3) | copy-start | bytes 9220
  1288.4 19.1 %copy-start.18 = (bf16[32,768]{1,0:T(8,128)(2,1)}, bf16[32,768]{1,0:T(8,128)(2,1)S(1)}, u32[]{:S(2)}) copy-start(bf16[32,768]{1,0:T(8,128)(2,1)S(1)} %fusion.65) | copy-start | bytes 147460
  1288.5 6.0 collective-permute-start
  1338.7 87.6 %reduce-scatter.5.cloned.1.call-start = ((), (), s32[]{:S(2)}) async-start(), calls=%async_computation.5 | async-start | bytes 245760 | tf_op jit(solution)/shard_map/reduce_scatter | solution.py:174
  1344.7 49.9 %copy-start.7 = (bf16[32,6,64]{2,0,1:T(8,128)(2,1)S(1)}, bf16[32,6,64]{2,0,1:T(8,128)(2,1)}, u32[]{:S(2)}) copy-start(bf16[32,6,64]{2,0,1:T(8,128)(2,1)} %fusion.71) | copy-start | bytes 73732
  1392.3 3.7 copy-start.4
  1397.1 3.8 copy-start.1
  1402.6 23.7 %copy-start.19 = (bf16[32,768]{1,0:T(8,128)(2,1)S(1)}, bf16[32,768]{1,0:T(8,128)(2,1)}, u32[]{:S(2)}) copy-start(bf16[32,768]{1,0:T(8,128)(2,1)} %copy-done.18) | copy-start | bytes 147460
  1402.6 23.7 %copy-start.22 = (bf16[32,768]{1,0:T(8,128)(2,1)S(1)}, bf16[32,768]{1,0:T(8,128)(2,1)}, u32[]{:S(2)}) copy-start(bf16[32,768]{1,0:T(8,128)(2,1)} %copy-done.21) | copy-start | bytes 147460
  1402.6 23.7 %copy-start.29 = (f32[768]{0:T(1024)S(1)}, f32[768]{0:T(1024)}, u32[]{:S(2)}) copy-start(f32[768]{0:T(1024)} %copy-done.28) | copy-start | bytes 9220
  1402.6 23.7 %copy-start.31 = (f32[768]{0:T(1024)S(1)}, f32[768]{0:T(1024)}, u32[]{:S(2)}) copy-start(f32[768]{0:T(1024)} %copy-done.30) | copy-start | bytes 9220
  1402.6 23.7 %copy-start.33 = (pred[32]{0:T(512)(128)(4,1)S(1)}, pred[32]{0:T(512)(128)(4,1)}, u32[]{:S(2)}) copy-start(pred[32]{0:T(512)(128)(4,1)} %copy-done.32) | copy-start | bytes 100
  (14 other events, 23.7 us)
Sparse Core Ops, SparseCore 0:
  13.0 1182.2 all-reduce.2
  1265.8 21.6 reduce-scatter.2
  1404.5 21.7 reduce-scatter.4
Sparse Core Ops, SparseCore 1:
  16.3 54.4 all-gather.8
  1204.0 46.7 all-gather.4
  1338.7 50.8 all-gather.6
where the time goes:
time: 1440 us
  waiting for transfers between devices  1300 us (90%)
  local copies, waits for them, and re-layouts  51.2 us (4%)
  blocking collectives  25 us (2%)
  matrix products  21.4 us (1%)
  other arithmetic  19.8 us (1%)
  between operations  17.8 us (1%)
    unnamed x7, waiting for transfers between devices  1170 us
    all_gather x2, waiting for transfers between devices, attend(): lax.all_gather(fresh_kv, 'seq', axis=1, tiled=True)  84 us
    reduce_scatter x2, waiting for transfers between devices, run_layer(): lax.psum_scatter(lax.dot_general(weights_out, attended, (((0,), (1,)), ((...  42.8 us
  transfers between devices with their start and end apart: 7, of which 6 were waited for; matrix products, arithmetic and copies ran while one was open for 2% of the time, Pallas kernels for 0%

commit v1 on v0

--- a/solution.py
+++ b/solution.py
@@ -118,7 +118,10 @@
     mod_share = jnp.dot(time_features(timestep), mod_weight[0], preferred_element_type=jnp.float32)[
         0
     ]
-    modulate = lax.all_gather(mod_share, ("seq", "tp"), axis=0, tiled=True).reshape(6, model_width)
+    by_tp = lax.all_gather(mod_share[None, None, :], "tp", axis=0, tiled=True)
+    modulate = lax.all_gather(
+        jnp.pad(by_tp.reshape(1, 4, -1), ((0, 0), (0, 4), (0, 0))), "seq", axis=0, tiled=True
+    )[:, :4].reshape(6, model_width)
     my_rows = seq_rank * tok_rows + jnp.arange(tok_rows, dtype=jnp.int32)
     video = (my_rows >= TEXT)[:, None]
     bounds = jnp.cumsum(patch_lengths)

time: 1440 us -> 378 us (0.26)
  waiting for transfers between devices: 1300 us -> 185 us
  blocking collectives: 25 us -> 82.3 us
    unnamed x7 -> x5, waiting for transfers between devices: 1170 us -> 0.76 us
    all_gather x1, waiting for transfers between devices: 0.03 us -> 49.3 us  [attend(): lax.all_gather(stale_own, 'seq', axis=1, tiled=True)]
    all_gather x0 -> x1, blocking collectives: none -> 47.1 us  [local(): lax.all_gather(jnp.pad(by_tp.reshape(1, 4, -1), ((0, 0), (0, 4), (0, 0)))...]
  transfers between devices with their start and end apart: 7 -> 6, of which waited for: 6 -> 6; matrix products, arithmetic and copies ran while one was open for 2% -> 3% of each run, Pallas kernels for 0% -> 0%
where the time goes in v1:
time: 378 us; the launch traced here: 376 us
  waiting for transfers between devices  185 us (49%)
  blocking collectives  82.3 us (22%)
  local copies, waits for them, and re-layouts  47.8 us (13%)
  matrix products  23.4 us (6%)
  other arithmetic  19 us (5%)
  between operations  16.1 us (4%)
    all_gather x2, waiting for transfers between devices, attend(): lax.all_gather(fresh_kv, 'seq', axis=1, tiled=True)  88 us
    all_gather x1, waiting for transfers between devices, attend(): lax.all_gather(stale_own, 'seq', axis=1, tiled=True)  49.3 us
    all_gather x1, blocking collectives, local(): lax.all_gather(jnp.pad(by_tp.reshape(1, 4, -1), ((0, 0), (0, 4), (0, 0)))...  47.1 us
    reduce_scatter x2, waiting for transfers between devices, run_layer(): lax.psum_scatter(lax.dot_general(weights_out, attended, (((0,), (1,)), ((...  42.4 us
    all_gather x2, blocking collectives, run_layer(): lax.all_gather(incoming, 'tp', axis=1, tiled=True).astype(jnp.float32)  24.5 us
    unnamed x1, blocking collectives  10.7 us
    dot_general x2, matrix products, run_layer(): jnp.einsum('td,dcf->tcf', normed, weights_qkv, preferred_element_type=jnp...  8.79 us
    slice x4, local copies, waits for them, and re-layouts, merge_block(): fresh_keys = fresh_block[0].reshape(key_count, head_count, HEAD)  8.52 us
  transfers between devices with their start and end apart: 6, of which 6 were waited for; matrix products, arithmetic and copies ran while one was open for 3% of the time, Pallas kernels for 0%

profile of v1, /device:TPU:32, one launch (start us, length us, event | category | flops | bytes accessed | tf_op | source)
XLA Modules:
  0.0 375.5 jit_solution(1353841677514574803)
XLA Ops:
  11.3 10.7 %all-reduce.1 = f32[576]{0:T(1024)S(1)} all-reduce(f32[576]{0:T(1024)S(1)} %dynamic-update-slice), channel_id=2, replica_groups=mesh['section'=2,'seq'=32,'tp'=4] {'tp'}, use_global_device_ids=true, to_apply=%add.1 | all-reduce | flops 576 | bytes 4608
  22.1 47.1 %all_gather.23 = f32[32,8,144]{2,1,0:T(8,128)S(1)} all-gather(f32[1,8,144]{2,1,0:T(8,128)S(1)} %pad.4), channel_id=1, replica_groups=mesh['section'=2,'seq'=32,'tp'=4] {'seq'}, dimensions={0}, use_global_device_ids=true | all-gather | bytes 152064 | tf_op jit(solution)/shard_map/all_gather | solution.py:122
  69.5 12.3 %all_gather.24 = bf16[32,3072]{1,0:T(8,128)(2,1)S(1)} all-gather(bf16[32,768]{1,0:T(8,128)(2,1)} %param.9), channel_id=1, replica_groups=mesh['section'=2,'seq'=32,'tp'=4] {'tp'}, dimensions={1}, use_global_device_ids=true | all-gather | bytes 245760 | tf_op jit(solution)/shard_map/all_gather | solution.py:158
  82.2 4.4 %fusion.2 = f32[32,3,384]{2,0,1:T(8,128)S(1)} fusion(bf16[1,3072,3,384]{3,1,2,0:T(8,128)(2,1)} %param.10, bf16[32,3072]{1,0:T(8,128)(2,1)S(1)} %all_gather.24, f32[3072]{0:T(1024)S(1)} %bitcast.178, f32[3072]{0:T(1024)S(1)} %bitcast.180, f32[3072]{0:T(1024)S(1)} %bitcast.182, f32[3072]{0:T(1024)S(1)} %bitcast.176, f32[32]{0:T(128)S(1)} %add_rsqrt_fusion.5, ...), kind=kOutput, calls=%fused_computation.2 | convolution fusion | flops 227377152 | bytes 7471392 | tf_op jit(solution)/shard_map/td,dcf->tcf/dot_general | solution.py:165
  93.1 43.2 %all-gather.6.cloned.1.call-done = bf16[2,1024,384]{2,1,0:T(8,128)(2,1)} async-done(((bf16[2,32,384]{2,1,0:T(8,128)(2,1)}), bf16[2,1024,384]{2,1,0:T(8,128)(2,1)}) %all-gather.6.cloned.1.call-update) | async-done | bytes 1572880 | tf_op jit(solution)/shard_map/all_gather | solution.py:150
  136.2 2.4 fusion.128
  139.8 49.3 %all-gather.10.cloned.1.call-done = bf16[1,2,1024,384]{3,2,1,0:T(8,128)(2,1)} async-done(((bf16[1,2,32,384]{3,2,1,0:T(8,128)(2,1)}), bf16[1,2,1024,384]{3,2,1,0:T(8,128)(2,1)}) %all-gather.10.cloned.1.call-update) | async-done | bytes 1572880 | tf_op jit(solution)/shard_map/all_gather | solution.py:151
  189.1 2.7 fusion.127
  195.8 2.3 copy.167
  199.5 2.4 fusion.28
  201.9 2.3 copy.168
  204.2 1.8 fusion.15
  207.5 21.4 %reduce-scatter.3.cloned.1.call-done = bf16[768,32]{0,1:T(8,128)(2,1)} async-done(((bf16[3072,32]{0,1:T(8,128)(2,1)}), bf16[768,32]{0,1:T(8,128)(2,1)}) %reduce-scatter.3.cloned.1.call-update) | async-done | bytes 49168 | tf_op jit(solution)/shard_map/reduce_scatter | solution.py:177
  231.2 4.7 %collective-permute-done = bf16[32,768]{1,0:T(8,128)(2,1)S(1)} collective-permute-done((bf16[32,768]{1,0:T(8,128)(2,1)S(1)}, bf16[32,768]{1,0:T(8,128)(2,1)S(1)}, u32[]{:S(2)}, u32[]{:S(2)}) %collective-permute-start) | collective-permute-done | bytes 49184 | tf_op jit(solution)/shard_map/ppermute | solution.py:16
  236.5 12.2 %all_gather.27 = bf16[32,3072]{1,0:T(8,128)(2,1)S(1)} all-gather(bf16[32,768]{1,0:T(8,128)(2,1)S(1)} %collective-permute-done), channel_id=1, replica_groups=mesh['section'=2,'seq'=32,'tp'=4] {'tp'}, dimensions={1}, use_global_device_ids=true | all-gather | bytes 245760 | tf_op jit(solution)/shard_map/all_gather | solution.py:158
  249.1 4.4 %fusion = f32[32,3,384]{2,0,1:T(8,128)S(1)} fusion(bf16[1,3072,3,384]{3,1,2,0:T(8,128)(2,1)} %param.10, bf16[32,3072]{1,0:T(8,128)(2,1)S(1)} %all_gather.27, f32[32]{0:T(128)S(1)} %add_rsqrt_fusion.4, f32[32]{0:T(128)S(1)} %broadcast_multiply_fusion.7, f32[3072]{0:T(1024)S(1)} %bitcast.179, f32[3072]{0:T(1024)S(1)} %bitcast.181, f32[3072]{0:T(1024)S(1)} %bitcast.183, ...), kind=kOutput, calls=%fused_computation | convolution fusion | flops 227377152 | bytes 7471392 | tf_op jit(solution)/shard_map/td,dcf->tcf/dot_general | solution.py:165
  260.0 1.4 multiply_reduce_fusion.2
  264.9 1.6 mul.479
  266.5 1.5 sub.161.clone
  268.0 1.6 sub.163
  269.6 1.5 sub.165
  271.0 1.6 sub.169
  272.7 1.5 fusion.93
  284.7 1.5 fusion.71
  286.2 44.9 %all-gather.8.cloned.1.call-done = bf16[2,1024,384]{2,1,0:T(8,128)(2,1)} async-done(((bf16[2,32,384]{2,1,0:T(8,128)(2,1)}), bf16[2,1024,384]{2,1,0:T(8,128)(2,1)}) %all-gather.8.cloned.1.call-update) | async-done | bytes 1572880 | tf_op jit(solution)/shard_map/all_gather | solution.py:150
  331.0 2.6 fusion.126
  333.7 2.3 copy.180
  338.6 2.4 copy.181
  340.9 1.5 fusion.17
  342.4 1.5 fusion.29
  346.5 21.0 %reduce-scatter.5.cloned.1.call-done = bf16[768,32]{0,1:T(8,128)(2,1)} async-done(((bf16[3072,32]{0,1:T(8,128)(2,1)}), bf16[768,32]{0,1:T(8,128)(2,1)}) %reduce-scatter.5.cloned.1.call-update) | async-done | bytes 49168 | tf_op jit(solution)/shard_map/reduce_scatter | solution.py:177
  367.5 1.5 fusion.77
  (222 shorter events, 46.0 us)
Async XLA Ops:
  7.2 199.0 %copy-start = (bf16[1,384,3072]{2,1,0:T(8,128)(2,1)S(1)}, bf16[1,384,3072]{2,1,0:T(8,128)(2,1)}, u32[]{:S(2)}) copy-start(bf16[1,384,3072]{2,1,0:T(8,128)(2,1)} %param.12) | copy-start | bytes 7077892
  7.2 129.0 %all-gather.6.cloned.1.call-start = ((), (), s32[]{:S(2)}) async-start(), calls=%async_computation.2 | async-start | bytes 1622016 | tf_op jit(solution)/shard_map/all_gather | solution.py:150
  7.3 241.8 %copy-start.28 = (pred[32]{0:T(512)(128)(4,1)}, pred[32]{0:T(512)(128)(4,1)S(1)}, u32[]{:S(2)}) copy-start(pred[32]{0:T(512)(128)(4,1)S(1)} %fusion.119) | copy-start | bytes 100
  86.6 2.9 copy-start.34
  87.6 4.7 %copy-start.36 = (s32[4]{0:T(128)S(1)}, s32[4]{0:T(128)}, u32[]{:S(2)}) copy-start(s32[4]{0:T(128)} %param.15) | copy-start | bytes 52
  88.4 50.2 %copy-start.31 = (f32[64]{0:T(128)}, f32[64]{0:T(128)S(1)}, u32[]{:S(2)}) copy-start(f32[64]{0:T(128)S(1)} %get-tuple-element.47) | copy-start | bytes 772
  88.5 4.3 %copy-start.30 = (f32[384]{0:T(512)}, f32[384]{0:T(512)S(1)}, u32[]{:S(2)}) copy-start(f32[384]{0:T(512)S(1)} %mul.449) | copy-start | bytes 4612
  88.6 4.2 %copy-start.23 = (f32[384]{0:T(512)}, f32[384]{0:T(512)S(1)}, u32[]{:S(2)}) copy-start(f32[384]{0:T(512)S(1)} %mul.459) | copy-start | bytes 4612
  88.9 49.7 %copy-start.33 = (pred[384]{0:T(512)(128)(4,1)}, pred[384]{0:T(512)(128)(4,1)S(1)}, u32[]{:S(2)}) copy-start(pred[384]{0:T(512)(128)(4,1)S(1)} %fusion.111) | copy-start | bytes 1156
  89.9 3.1 copy-start.8
  90.0 3.1 copy-start.9
  90.1 3.0 copy-start.6
  90.2 2.9 copy-start.7
  90.9 98.2 %all-gather.10.cloned.1.call-start = ((), (), s32[]{:S(2)}) async-start(), calls=%async_computation.6 | async-start | bytes 1622016 | tf_op jit(solution)/shard_map/all_gather | solution.py:151
  91.7 137.3 %reduce-scatter.3.cloned.1.call-start = ((), (), s32[]{:S(2)}) async-start(), calls=%async_computation.3 | async-start | bytes 245760 | tf_op jit(solution)/shard_map/reduce_scatter | solution.py:177
  92.9 111.3 %copy-start.2 = (pred[32,1024]{1,0:T(8,128)(4,1)}, pred[32,1024]{1,0:T(8,128)(4,1)S(1)}, u32[]{:S(2)}) copy-start(pred[32,1024]{1,0:T(8,128)(4,1)S(1)} %broadcast_compare_fusion) | copy-start | bytes 98308
  204.2 24.8 %copy-start.16 = (bf16[32,768]{1,0:T(8,128)(2,1)S(1)}, bf16[32,768]{1,0:T(8,128)(2,1)}, u32[]{:S(2)}) copy-start(bf16[32,768]{1,0:T(8,128)(2,1)} %param.9) | copy-start | bytes 147460
  207.3 123.7 %all-gather.8.cloned.1.call-start = ((), (), s32[]{:S(2)}) async-start(), calls=%async_computation.4 | async-start | bytes 1622016 | tf_op jit(solution)/shard_map/all_gather | solution.py:150
  207.5 41.5 %copy-start.24 = (f32[768]{0:T(1024)}, f32[768]{0:T(1024)S(1)}, u32[]{:S(2)}) copy-start(f32[768]{0:T(1024)S(1)} %get-tuple-element.2) | copy-start | bytes 9220
  207.5 41.5 %copy-start.26 = (f32[768]{0:T(1024)}, f32[768]{0:T(1024)S(1)}, u32[]{:S(2)}) copy-start(f32[768]{0:T(1024)S(1)} %get-tuple-element.3) | copy-start | bytes 9220
  229.9 19.2 %copy-start.14 = (bf16[32,768]{1,0:T(8,128)(2,1)}, bf16[32,768]{1,0:T(8,128)(2,1)S(1)}, u32[]{:S(2)}) copy-start(bf16[32,768]{1,0:T(8,128)(2,1)S(1)} %fusion.65) | copy-start | bytes 147460
  229.9 6.0 %collective-permute-start = (bf16[32,768]{1,0:T(8,128)(2,1)S(1)}, bf16[32,768]{1,0:T(8,128)(2,1)S(1)}, u32[]{:S(2)}, u32[]{:S(2)}) collective-permute-start(bf16[32,768]{1,0:T(8,128)(2,1)S(1)} %fusion.65), channel_id=1, source_target_pairs={{0,128},{1,129},{2,130},{3,131},{4,132},{5,133},{6,134},{7,135},{8... | collective-permute-start | bytes 147464 | tf_op jit(solution)/shard_map/ppermute | solution.py:16
  280.1 87.3 %reduce-scatter.5.cloned.1.call-start = ((), (), s32[]{:S(2)}) async-start(), calls=%async_computation.5 | async-start | bytes 245760 | tf_op jit(solution)/shard_map/reduce_scatter | solution.py:177
  286.2 49.8 %copy-start.5 = (bf16[32,6,64]{2,0,1:T(8,128)(2,1)S(1)}, bf16[32,6,64]{2,0,1:T(8,128)(2,1)}, u32[]{:S(2)}) copy-start(bf16[32,6,64]{2,0,1:T(8,128)(2,1)} %fusion.71) | copy-start | bytes 73732
  333.7 3.7 copy-start.3
  338.5 3.8 %copy-start.1 = (f32[6,32,1024]{2,1,0:T(8,128)S(1)}, f32[6,32,1024]{2,1,0:T(8,128)}, u32[]{:S(2)}) copy-start(f32[6,32,1024]{2,1,0:T(8,128)} %get-tuple-element.54) | copy-start | bytes 2359300
  340.9 3.0 copy-start.4
  344.0 23.5 %copy-start.15 = (bf16[32,768]{1,0:T(8,128)(2,1)S(1)}, bf16[32,768]{1,0:T(8,128)(2,1)}, u32[]{:S(2)}) copy-start(bf16[32,768]{1,0:T(8,128)(2,1)} %copy-done.14) | copy-start | bytes 147460
  344.0 23.5 %copy-start.18 = (bf16[32,768]{1,0:T(8,128)(2,1)S(1)}, bf16[32,768]{1,0:T(8,128)(2,1)}, u32[]{:S(2)}) copy-start(bf16[32,768]{1,0:T(8,128)(2,1)} %copy-done.17) | copy-start | bytes 147460
  344.0 23.4 %copy-start.25 = (f32[768]{0:T(1024)S(1)}, f32[768]{0:T(1024)}, u32[]{:S(2)}) copy-start(f32[768]{0:T(1024)} %copy-done.24) | copy-start | bytes 9220
  344.0 23.4 %copy-start.27 = (f32[768]{0:T(1024)S(1)}, f32[768]{0:T(1024)}, u32[]{:S(2)}) copy-start(f32[768]{0:T(1024)} %copy-done.26) | copy-start | bytes 9220
  344.0 23.4 %copy-start.29 = (pred[32]{0:T(512)(128)(4,1)S(1)}, pred[32]{0:T(512)(128)(4,1)}, u32[]{:S(2)}) copy-start(pred[32]{0:T(512)(128)(4,1)} %copy-done.28) | copy-start | bytes 100
  (11 other events, 14.1 us)
Sparse Core Ops, SparseCore 0:
  91.1 45.1 all-gather.5
  138.8 50.2 all-gather.9
  207.5 21.4 reduce-scatter.2
  280.2 50.7 all-gather.7
  345.9 21.4 reduce-scatter.4

commit v2 on v0

v2 whole, which is shorter than its diff:
```python
import math

import jax
import jax.numpy as jnp
from jax import lax
from jax.experimental import pallas as pl
from jax.experimental.pallas import tpu as pltpu
from jax.sharding import PartitionSpec as P

HEAD = 64
TEMB = 512
TEXT = 226


def patch_index(index, bounds):
    video_row = index - TEXT
    patch_id = jnp.sum((video_row[:, None] >= bounds[None, :-1]).astype(jnp.int32), axis=1)
    return jnp.where(index < TEXT, 0, patch_id)


def time_features(timestep):
    half_width = TEMB // 2
    frequency = jnp.exp(
        -math.log(10000.0) * jnp.arange(half_width).astype(jnp.float32) / half_width
    )
    phases = timestep.astype(jnp.float32)[:, None] * frequency[None, :]
    embedded = jnp.concatenate([jnp.cos(phases), jnp.sin(phases)], axis=1)
    return jax.nn.silu(embedded).astype(jnp.bfloat16)


def axis_freq(dim_size):
    return 1.0 / 10000.0 ** (jnp.arange(0, dim_size, 2).astype(jnp.float32) / dim_size)


def rope_tables(positions, head_count):
    coords = positions.astype(jnp.float32)
    angles = jnp.concatenate(
        [
            coords[0][:, None] * axis_freq(HEAD // 4)[None, :],
            coords[1][:, None] * axis_freq(3 * HEAD // 8)[None, :],
            coords[2][:, None] * axis_freq(3 * HEAD // 8)[None, :],
        ],
        axis=1,
    )
    angles = jnp.repeat(angles, 2, axis=1)
    return (jnp.tile(jnp.cos(angles), (1, head_count)), jnp.tile(jnp.sin(angles), (1, head_count)))


MESH = pl.DeviceIdType.MESH
OTHERS = (1, 3, 2)
VMEM_SPEC = pl.BlockSpec(memory_space=pltpu.VMEM)


def place():
    seq = lax.axis_index("seq")
    return seq // 8, (seq // 2) % 4, seq % 2


def seq_of(x, z, c):
    return (x * 4 + z) * 2 + c


def remote(source, target, send_sem, recv_sem, device):
    return pltpu.make_async_remote_copy(
        src_ref=source,
        dst_ref=target,
        send_sem=send_sem,
        recv_sem=recv_sem,
        device_id=device,
        device_id_type=MESH,
    )


def seq_peers():
    x, z, c = place()
    along_z = [{"seq": seq_of(x, (z + d) % 4, c)} for d in OTHERS]
    along_x = [{"seq": seq_of((x + d) % 4, z, c)} for d in OTHERS]
    return along_z + along_x + [{"seq": seq_of(x, z, 1 - c)}]


def tp_peers():
    tp = lax.axis_index("tp")
    return [{"tp": (tp + d) % 4} for d in OTHERS]


def greet(peers):
    barrier = pltpu.get_barrier_semaphore()
    for peer in peers:
        pl.semaphore_signal(barrier, inc=1, device_id=peer, device_id_type=MESH)
    pl.semaphore_wait(barrier, len(peers))


class SeqGather:
    def __init__(self, own, blocks, send_sems, recv_sems):
        self.own, self.blocks = own, blocks
        self.send_sems, self.recv_sems = send_sems, recv_sems

    def send(self, slot, source, x, z, c, device):
        remote(
            source,
            self.blocks.at[x, z, c],
            self.send_sems.at[slot],
            self.recv_sems.at[x, z, c],
            device,
        ).start()

    def arrived(self, x, z, c):
        block = self.blocks.at[x, z, c]
        remote(
            block, block, self.send_sems.at[0], self.recv_sems.at[x, z, c], seq_peers()[-1]
        ).wait_recv()

    def start(self):
        x, z, c = place()
        for k, peer in enumerate(seq_peers()):
            self.send(k, self.own, x, z, c, peer)

    def forward_z(self):
        x, z, c = place()
        peers = seq_peers()
        for i, d in enumerate(OTHERS):
            from_z = (z + d) % 4
            self.arrived(x, from_z, c)
            for k, peer in enumerate(peers[3:]):
                self.send(7 + 4 * i + k, self.blocks.at[x, from_z, c], x, from_z, c, peer)

    def forward_x(self):
        x, z, c = place()
        partner = seq_peers()[-1]
        for i, dz in enumerate((0,) + OTHERS):
            for k, dx in enumerate(OTHERS):
                from_x, from_z = (x + dx) % 4, (z + dz) % 4
                self.arrived(from_x, from_z, c)
                block = self.blocks.at[from_x, from_z, c]
                self.send(19 + 3 * i + k, block, from_x, from_z, c, partner)

    def finish(self):
        x, z, c = place()
        for dz in (0,) + OTHERS:
            for dx in (0,) + OTHERS:
                self.arrived((x + dx) % 4, (z + dz) % 4, 1 - c)

    def drain(self):
        x, z, c = place()
        block = self.blocks.at[x, z, c]
        for slot in range(GATHER_SENDS):
            remote(
                block, block, self.send_sems.at[slot], self.recv_sems.at[x, z, c], seq_peers()[-1]
            ).wait_send()


GATHER_SENDS = 7 + 12 + 12


def modulation_kernel(share_ref, out_ref, local_sem, tp_send, tp_recv, send_sems, recv_sems):
    x, z, c = place()
    tp = lax.axis_index("tp")
    greet(seq_peers() + tp_peers())
    own = out_ref.at[x, z, c]
    keep = pltpu.make_async_copy(share_ref, own.at[tp], local_sem)
    keep.start()
    copies = []
    for k, peer in enumerate(tp_peers()):
        copy = remote(share_ref, own.at[tp], tp_send.at[k], tp_recv.at[tp], peer)
        copy.start()
        copies.append(copy)
    keep.wait()
    for k, d in enumerate(OTHERS):
        source = (tp + d) % 4
        remote(
            share_ref, own.at[source], tp_send.at[k], tp_recv.at[source], tp_peers()[k]
        ).wait_recv()
    gather = SeqGather(own, out_ref, send_sems, recv_sems)
    gather.start()
    gather.forward_z()
    gather.forward_x()
    gather.finish()
    for copy in copies:
        copy.wait_send()
    gather.drain()


def gather_modulation(share):
    cols = share.shape[-1]
    return pl.pallas_call(
        modulation_kernel,
        out_shape=jax.ShapeDtypeStruct((4, 4, 2, 4, 1, cols), jnp.float32),
        in_specs=[VMEM_SPEC],
        out_specs=VMEM_SPEC,
        scratch_shapes=[
            pltpu.SemaphoreType.DMA,
            pltpu.SemaphoreType.DMA((3,)),
            pltpu.SemaphoreType.DMA((4,)),
            pltpu.SemaphoreType.DMA((GATHER_SENDS,)),
            pltpu.SemaphoreType.DMA((4, 4, 2)),
        ],
        compiler_params=pltpu.CompilerParams(collective_id=0, has_side_effects=True),
    )(share)


def head_norm_rope(values, gain, cosine, sine):
    lane = lax.broadcasted_iota(jnp.int32, (values.shape[0], 128), 1)
    low = lane < HEAD
    groups = []
    for g in range(values.shape[1] // 128):
        part = values[:, g * 128 : (g + 1) * 128]

        def average(t):
            first = jnp.sum(jnp.where(low, t, 0.0), axis=1, keepdims=True)
            second = jnp.sum(jnp.where(low, 0.0, t), axis=1, keepdims=True)
            return jnp.where(low, first, second) * (1.0 / HEAD)

        centred = part - average(part)
        unit = centred * lax.rsqrt(average(centred * centred) + 1e-06)
        unit = unit * gain[:, g * 128 : (g + 1) * 128]
        turned = jnp.where(lane % 2 == 0, pltpu.roll(unit, 127, 1), pltpu.roll(unit, 1, 1))
        cos_part = cosine[:, g * 128 : (g + 1) * 128]
        groups.append(unit * cos_part + turned * sine[:, g * 128 : (g + 1) * 128])
    return jnp.concatenate(groups, axis=1)


def layer_kernel(
    hidden_ref,
    w_qkv_hbm,
    w_out_hbm,
    stale_ref,
    mod_ref,
    gain_ref,
    cos_ref,
    sin_ref,
    video_ref,
    limit_ref,
    out_ref,
    kv_ref,
    w_qkv,
    w_out,
    x_all,
    stale_all,
    fresh_all,
    partial,
    reduced,
    w_sems,
    x_send,
    x_recv,
    pass_send,
    r_send,
    r_recv,
    stale_send,
    stale_recv,
    fresh_send,
    fresh_recv,
):
    x, z, c = place()
    tp = lax.axis_index("tp")
    section = lax.axis_index("section")
    rows, share = hidden_ref.shape
    head_cols = w_qkv.shape[2]
    heads = head_cols // HEAD
    load_qkv = pltpu.make_async_copy(w_qkv_hbm, w_qkv, w_sems.at[0])
    load_out = pltpu.make_async_copy(w_out_hbm, w_out, w_sems.at[1])
    load_qkv.start()
    load_out.start()
    across = [{"section": 1 - section, "tp": (tp + d) % 4} for d in (0,) + OTHERS]
    greet(tp_peers() + seq_peers() + across)

    @pl.when(section == 0)
    def _():
        for k, peer in enumerate(tp_peers()):
            remote(hidden_ref, x_all.at[tp], x_send.at[k], x_recv.at[tp], peer).start()
        x_all[tp] = hidden_ref[...]

    stale = SeqGather(stale_ref, stale_all, stale_send, stale_recv)
    stale.start()
    stale_all[x, z, c] = stale_ref[...]

    def x_arrived(source):
        remote(
            hidden_ref, x_all.at[source], x_send.at[0], x_recv.at[source], tp_peers()[0]
        ).wait_recv()

    @pl.when(section == 1)
    def _():
        stale.forward_z()
        stale.forward_x()
        stale.finish()
        x_arrived(tp)

    for d in OTHERS:
        x_arrived((tp + d) % 4)

    video = video_ref[...] > 0.0
    width = share * 4
    total = jnp.zeros((rows, 1), jnp.float32)
    for t in range(4):
        total += jnp.sum(x_all[t].astype(jnp.float32), axis=1, keepdims=True)
    mean = total * (1.0 / width)
    square = jnp.zeros((rows, 1), jnp.float32)
    for t in range(4):
        centred = x_all[t].astype(jnp.float32) - mean
        square += jnp.sum(centred * centred, axis=1, keepdims=True)
    inverse = lax.rsqrt(square * (1.0 / width) + 1e-05)

    @pl.when(section == 0)
    def _():
        stale.forward_z()

    load_qkv.wait()
    proj = [jnp.zeros((rows, head_cols), jnp.float32) for _ in range(3)]
    for t in range(4):
        cols = slice(t * share, (t + 1) * share)
        shift = jnp.where(video, mod_ref[0:1, cols], mod_ref[3:4, cols])
        scale = jnp.where(video, mod_ref[1:2, cols], mod_ref[4:5, cols])
        centred = x_all[t].astype(jnp.float32) - mean
        normed = (centred * inverse * (1.0 + scale) + shift).astype(jnp.bfloat16)
        for part in (1, 2, 0):
            proj[part] += jnp.dot(normed, w_qkv[part, cols, :], preferred_element_type=jnp.float32)
    cosine, sine = cos_ref[...], sin_ref[...]
    keys = head_norm_rope(proj[1], gain_ref[1:2, :], cosine, sine).astype(jnp.bfloat16)
    kv_ref[0] = keys
    kv_ref[1] = proj[2].astype(jnp.bfloat16)
    fresh_all[x, z, c, 0] = keys
    fresh_all[x, z, c, 1] = proj[2].astype(jnp.bfloat16)
    fresh = SeqGather(kv_ref, fresh_all, fresh_send, fresh_recv)
    fresh.start()

    @pl.when(section == 0)
    def _():
        stale.forward_x()

    queries = head_norm_rope(proj[0], gain_ref[0:1, :], cosine, sine)
    stacked = jnp.concatenate([queries] * heads, axis=0)
    row_head = lax.broadcasted_iota(jnp.int32, stacked.shape, 0) // rows
    col_head = lax.broadcasted_iota(jnp.int32, stacked.shape, 1) // HEAD
    spread = jnp.where(row_head == col_head, stacked, 0.0).astype(jnp.bfloat16)
    fresh.forward_z()

    @pl.when(section == 0)
    def _():
        stale.finish()

    tokens = rows * 32

    def all_rows(blocks, which):
        return blocks[:, :, :, which].reshape(tokens, head_cols)

    contract = (((1,), (1,)), ((), ()))
    scores_stale = lax.dot_general(
        spread, all_rows(stale_all, 0), contract, preferred_element_type=jnp.float32
    )
    fresh.forward_x()
    fresh.finish()
    scores_fresh = lax.dot_general(
        spread, all_rows(fresh_all, 0), contract, preferred_element_type=jnp.float32
    )
    column = lax.broadcasted_iota(jnp.int32, scores_fresh.shape, 1)
    allowed = column < limit_ref[...]
    scores = jnp.where(allowed, scores_fresh, scores_stale) * HEAD ** (-0.5)
    weights = jnp.exp(scores - jnp.max(scores, axis=1, keepdims=True))
    denominator = jnp.sum(weights, axis=1, keepdims=True)
    part_fresh = jnp.where(allowed, weights, 0.0).astype(jnp.bfloat16)
    part_stale = jnp.where(allowed, 0.0, weights).astype(jnp.bfloat16)
    mixed = jnp.dot(part_fresh, all_rows(fresh_all, 1), preferred_element_type=jnp.float32)
    mixed += jnp.dot(part_stale, all_rows(stale_all, 1), preferred_element_type=jnp.float32)
    mixed = jnp.where(row_head == col_head, mixed / denominator, 0.0)
    attended = mixed[0:rows]
    for h in range(1, heads):
        attended += mixed[h * rows : (h + 1) * rows]
    attended = attended.astype(jnp.bfloat16)

    load_out.wait()
    for t in range(4):
        partial[t] = jnp.dot(
            attended, w_out[:, t * share : (t + 1) * share], preferred_element_type=jnp.float32
        ).astype(jnp.bfloat16)
    r_copies = []
    for k, d in enumerate(OTHERS):
        target = (tp + d) % 4
        copy = remote(
            partial.at[target], reduced.at[tp], r_send.at[k], r_recv.at[tp], {"tp": target}
        )
        copy.start()
        r_copies.append(copy)
    mine = pl.ds(pl.multiple_of(tp * share, 128), share)
    gate = jnp.where(video, mod_ref[2:3, mine], mod_ref[5:6, mine])
    projected = partial[tp].astype(jnp.float32)
    for k, d in enumerate(OTHERS):
        source = (tp + d) % 4
        remote(
            partial.at[source], reduced.at[source], r_send.at[k], r_recv.at[source], {"tp": source}
        ).wait_recv()
        projected += reduced[source].astype(jnp.float32)
    out_ref[...] = (x_all[tp].astype(jnp.float32) + gate * projected).astype(jnp.bfloat16)

    @pl.when(section == 0)
    def _():
        passes = []
        for k, peer in enumerate(across):
            copy = remote(out_ref, x_all.at[tp], pass_send.at[k], x_recv.at[tp], peer)
            copy.start()
            passes.append(copy)
        for k, peer in enumerate(tp_peers()):
            remote(hidden_ref, x_all.at[tp], x_send.at[k], x_recv.at[tp], peer).wait_send()
        for copy in passes:
            copy.wait_send()

    for copy in r_copies:
        copy.wait_send()
    stale.drain()
    fresh.drain()


def run_layers(hidden, w_qkv, w_out, stale, modulate, gains, cosine, sine, video, limits):
    rows, share = hidden.shape
    head_cols = w_out.shape[0]
    blocks = pltpu.VMEM((4, 4, 2, 2, rows, head_cols), jnp.bfloat16)
    dma = pltpu.SemaphoreType.DMA
    any_spec = pl.BlockSpec(memory_space=pl.ANY)
    return pl.pallas_call(
        layer_kernel,
        out_shape=(
            jax.ShapeDtypeStruct((rows, share), jnp.bfloat16),
            jax.ShapeDtypeStruct((2, rows, head_cols), jnp.bfloat16),
        ),
        in_specs=[VMEM_SPEC, any_spec, any_spec] + [VMEM_SPEC] * 7,
        out_specs=(VMEM_SPEC, VMEM_SPEC),
        scratch_shapes=[
            pltpu.VMEM(w_qkv.shape, jnp.bfloat16),
            pltpu.VMEM(w_out.shape, jnp.bfloat16),
            pltpu.VMEM((4, rows, share), jnp.bfloat16),
            blocks,
            blocks,
            pltpu.VMEM((4, rows, share), jnp.bfloat16),
            pltpu.VMEM((4, rows, share), jnp.bfloat16),
            dma((2,)),
            dma((3,)),
            dma((4,)),
            dma((4,)),
            dma((3,)),
            dma((4,)),
            dma((GATHER_SENDS,)),
            dma((4, 4, 2)),
            dma((GATHER_SENDS,)),
            dma((4, 4, 2)),
        ],
        compiler_params=pltpu.CompilerParams(collective_id=1, has_side_effects=True),
    )(hidden, w_qkv, w_out, stale, modulate, gains, cosine, sine, video, limits)


def local(
    hidden,
    qkv_weight,
    qk_gain,
    out_weight,
    mod_weight,
    stale_kv,
    patch_lengths,
    positions,
    timestep,
):
    tok_rows = hidden.shape[0]
    head_count = qkv_weight.shape[3] // HEAD
    seq_rank = lax.axis_index("seq")
    share = jnp.dot(time_features(timestep), mod_weight[0], preferred_element_type=jnp.float32)
    modulate = gather_modulation(share).reshape(6, -1)
    my_rows = seq_rank * tok_rows + jnp.arange(tok_rows, dtype=jnp.int32)
    video = (my_rows >= TEXT)[:, None]
    bounds = jnp.cumsum(patch_lengths)
    query_patch = patch_index(my_rows, bounds)
    ends = jnp.where(jnp.arange(bounds.shape[0]) == bounds.shape[0] - 1, 1 << 30, TEXT + bounds)
    is_patch = query_patch[:, None] == jnp.arange(bounds.shape[0])[None, :]
    limits = jnp.sum(jnp.where(is_patch, ends[None, :], 0), axis=1, keepdims=True)
    limits = jnp.tile(limits.astype(jnp.int32), (head_count, 1))
    cosine, sine = rope_tables(positions, head_count)
    even = jnp.arange(cosine.shape[1]) % 2 == 0
    cosine = jnp.where(video, cosine, 1.0)
    sine = jnp.where(video, jnp.where(even, -sine, sine), 0.0)
    result, fresh_kv = run_layers(
        hidden,
        jnp.transpose(qkv_weight[0], (1, 0, 2)),
        out_weight[0],
        stale_kv[0],
        modulate,
        jnp.tile(qk_gain[0], (1, head_count)),
        cosine,
        sine,
        video.astype(jnp.float32),
        limits,
    )
    return (result[None], fresh_kv[None])


def solution(mesh):
    return jax.shard_map(
        local,
        mesh=mesh,
        in_specs=(
            P("seq", "tp"),
            P("section", None, None, "tp"),
            P("section", None, None),
            P("section", "tp", None),
            P("section", None, ("seq", "tp")),
            P("section", None, "seq", "tp"),
            P(),
            P(None, "seq"),
            P(),
        ),
        out_specs=(P("section", "seq", "tp"), P("section", None, "seq", "tp")),
        check_vma=False,
    )
```

time: 1440 us -> 99.2 us (0.07)
  waiting for transfers between devices: 1300 us -> 0 us
  Pallas kernels: 0 us -> 85.5 us
  local copies, waits for them, and re-layouts: 51.2 us -> 6.27 us
  blocking collectives: 25 us -> 0 us
  matrix products: 21.4 us -> 0.71 us
  between operations: 17.8 us -> 1.41 us
  other arithmetic: 19.8 us -> 4.6 us
    unnamed x7 -> x0, waiting for transfers between devices: 1170 us -> none
    pallas_call x0 -> x2, Pallas kernels: none -> 85.5 us  [the longest x1 63.8 us: run_layers(): pl.pallas_call(layer_kernel, out_shape=(jax.ShapeDtypeStruct((rows, share...]
    all_gather x3 -> x0, waiting for transfers between devices: 84 us -> none  [the longest x2 84 us: attend(): lax.all_gather(fresh_kv, 'seq', axis=1, tiled=True)]
    reduce_scatter x2 -> x0, waiting for transfers between devices: 42.8 us -> none  [run_layer(): lax.psum_scatter(lax.dot_general(weights_out, attended, (((0,), (1,)), ((...]
    all_gather x2 -> x0, blocking collectives: 25 us -> none  [run_layer(): lax.all_gather(incoming, 'tp', axis=1, tiled=True).astype(jnp.float32)]
    slice x17 -> x0, local copies, waits for them, and re-layouts: 24.4 us -> none  [the longest x4 9.92 us: merge_block(): fresh_keys = fresh_block[0].reshape(key_count, head_count, HEAD)]
    dot_general x12 -> x0, matrix products: 20.3 us -> none  [the longest x2 8.78 us: run_layer(): jnp.einsum('td,dcf->tcf', normed, weights_qkv, preferred_element_type=jnp...]
  transfers between devices with their start and end apart: 7 -> 0, of which waited for: 6 -> 0; matrix products, arithmetic and copies ran while one was open for 2% -> 0% of each run, Pallas kernels for 0% -> 0%
where the time goes in v2:
time: 99.2 us; the launch traced here: 98.5 us
  Pallas kernels  85.5 us (86%)
  local copies, waits for them, and re-layouts  6.27 us (6%)
  other arithmetic  4.6 us (5%)
  between operations  1.41 us (1%)
    pallas_call x1, Pallas kernels, run_layers(): pl.pallas_call(layer_kernel, out_shape=(jax.ShapeDtypeStruct((rows, share...  63.8 us
    pallas_call x1, Pallas kernels, gather_modulation(): pl.pallas_call(modulation_kernel, out_shape=jax.ShapeDtypeStruct((4, 4, 2...  21.7 us
    unnamed x4, local copies, waits for them, and re-layouts  3 us

profile of v2, /device:TPU:32, one launch (start us, length us, event | category | flops | bytes accessed | tf_op | source)
XLA Modules:
  0.0 98.5 jit_solution(6347042345805615975)
XLA Ops:
  0.6 0.0 copy-start
  1.4 0.2 copy-done
  1.6 0.7 fusion.share_ref
  2.3 21.7 %shard_map.104 = f32[4,4,2,4,1,144]{5,4,3,2,1,0:T(1,128)} custom-call(f32[1,144]{1,0:T(1,128)} %fusion.share_ref), custom_call_target="tpu_custom_call" | custom-call | tf_op jit(solution)/shard_map/pallas_call | solution.py:185
  24.0 1.3 %reduce = f32[4,4,2,4,144]{4,3,2,1,0:T(4,128)S(1)} reduce(f32[4,4,2,4,1,144]{5,4,3,2,1,0:T(1,128)} %shard_map.104, f32[]{:T(128)} %constant.70), dimensions={4}, to_apply=%pallas_call.10.reduce_sub_computation | reduce | bytes 147460 | tf_op jit(solution)/shard_map/pallas_call | solution.py:185
  25.2 0.8 reshape.131.mod_ref
  26.0 0.7 tile.37
  26.7 0.7 tile.38.gain_ref
  27.4 0.7 convert_element_type.47
  28.1 0.1 broadcast_multiply_fusion.1
  28.2 0.1 broadcast_multiply_fusion.2
  28.2 0.1 fusion.4
  28.3 0.1 copy.15
  28.4 0.1 tile.42
  28.6 0.1 copy.14
  28.6 0.1 tile.40
  28.7 0.7 fusion.2
  29.4 0.6 fusion.3.video_ref
  30.0 0.8 reduce-window.4
  30.9 0.1 convert_reduce_fusion
  31.0 0.1 select_reduce_fusion
  31.1 0.8 tile.45.limit_ref
  31.8 63.8 %shard_map.105 = (bf16[32,768]{1,0:T(8,128)(2,1)}, bf16[2,32,384]{2,1,0:T(8,128)(2,1)}) custom-call(bf16[32,768]{1,0:T(8,128)(2,1)} %hidden_ref.1, bf16[3,3072,384]{2,1,0:T(8,128)(2,1)} %bitcast.27, bf16[384,3072]{1,0:T(8,128)(2,1)} %bitcast.28, bf16[2,32,384]{2,1,0:T(8,128)(2,1)} %bitcast.31, f32[6,3072]{1,0:T(8,128)} %reshape.131.mod_ref, ...), custom_call_target="tpu_custom_call" | custom-call | tf_op jit(solution)/shard_map/pallas_call | solution.py:418
  95.6 1.4 %copy.20 = bf16[1,32,768]{2,1,0:T(8,128)(2,1)} copy(bf16[1,32,768]{2,1,0:T(8,128)(2,1)} %bitcast.33) | data formatting | bytes 98304
  97.1 1.4 %copy.21 = bf16[1,2,32,384]{3,2,1,0:T(8,128)(2,1)} copy(bf16[1,2,32,384]{3,2,1,0:T(8,128)(2,1)} %bitcast.32) | data formatting | bytes 98304
  (17 shorter events, 0.2 us)
Async XLA Ops:
  0.6 0.9 copy-start

commit v3 on v2

--- a/solution.py
+++ b/solution.py
@@ -12,12 +12,6 @@
 TEXT = 226
 
 
-def patch_index(index, bounds):
-    video_row = index - TEXT
-    patch_id = jnp.sum((video_row[:, None] >= bounds[None, :-1]).astype(jnp.int32), axis=1)
-    return jnp.where(index < TEXT, 0, patch_id)
-
-
 def time_features(timestep):
     half_width = TEMB // 2
     frequency = jnp.exp(
@@ -26,24 +20,6 @@
     phases = timestep.astype(jnp.float32)[:, None] * frequency[None, :]
     embedded = jnp.concatenate([jnp.cos(phases), jnp.sin(phases)], axis=1)
     return jax.nn.silu(embedded).astype(jnp.bfloat16)
-
-
-def axis_freq(dim_size):
-    return 1.0 / 10000.0 ** (jnp.arange(0, dim_size, 2).astype(jnp.float32) / dim_size)
-
-
-def rope_tables(positions, head_count):
-    coords = positions.astype(jnp.float32)
-    angles = jnp.concatenate(
-        [
-            coords[0][:, None] * axis_freq(HEAD // 4)[None, :],
-            coords[1][:, None] * axis_freq(3 * HEAD // 8)[None, :],
-            coords[2][:, None] * axis_freq(3 * HEAD // 8)[None, :],
-        ],
-        axis=1,
-    )
-    angles = jnp.repeat(angles, 2, axis=1)
-    return (jnp.tile(jnp.cos(angles), (1, head_count)), jnp.tile(jnp.sin(angles), (1, head_count)))
 
 
 MESH = pl.DeviceIdType.MESH
@@ -110,10 +86,19 @@
             block, block, self.send_sems.at[0], self.recv_sems.at[x, z, c], seq_peers()[-1]
         ).wait_recv()
 
+    def start_z(self):
+        x, z, c = place()
+        for k, peer in enumerate(seq_peers()[:3]):
+            self.send(k, self.own, x, z, c, peer)
+
+    def start_x(self):
+        x, z, c = place()
+        for k, peer in enumerate(seq_peers()[3:]):
+            self.send(3 + k, self.own, x, z, c, peer)
+
     def start(self):
-        x, z, c = place()
-        for k, peer in enumerate(seq_peers()):
-            self.send(k, self.own, x, z, c, peer)
+        self.start_z()
+        self.start_x()
 
     def forward_z(self):
         x, z, c = place()
@@ -152,52 +137,6 @@
 GATHER_SENDS = 7 + 12 + 12
 
 
-def modulation_kernel(share_ref, out_ref, local_sem, tp_send, tp_recv, send_sems, recv_sems):
-    x, z, c = place()
-    tp = lax.axis_index("tp")
-    greet(seq_peers() + tp_peers())
-    own = out_ref.at[x, z, c]
-    keep = pltpu.make_async_copy(share_ref, own.at[tp], local_sem)
-    keep.start()
-    copies = []
-    for k, peer in enumerate(tp_peers()):
-        copy = remote(share_ref, own.at[tp], tp_send.at[k], tp_recv.at[tp], peer)
-        copy.start()
-        copies.append(copy)
-    keep.wait()
-    for k, d in enumerate(OTHERS):
-        source = (tp + d) % 4
-        remote(
-            share_ref, own.at[source], tp_send.at[k], tp_recv.at[source], tp_peers()[k]
-        ).wait_recv()
-    gather = SeqGather(own, out_ref, send_sems, recv_sems)
-    gather.start()
-    gather.forward_z()
-    gather.forward_x()
-    gather.finish()
-    for copy in copies:
-        copy.wait_send()
-    gather.drain()
-
-
-def gather_modulation(share):
-    cols = share.shape[-1]
-    return pl.pallas_call(
-        modulation_kernel,
-        out_shape=jax.ShapeDtypeStruct((4, 4, 2, 4, 1, cols), jnp.float32),
-        in_specs=[VMEM_SPEC],
-        out_specs=VMEM_SPEC,
-        scratch_shapes=[
-            pltpu.SemaphoreType.DMA,
-            pltpu.SemaphoreType.DMA((3,)),
-            pltpu.SemaphoreType.DMA((4,)),
-            pltpu.SemaphoreType.DMA((GATHER_SENDS,)),
-            pltpu.SemaphoreType.DMA((4, 4, 2)),
-        ],
-        compiler_params=pltpu.CompilerParams(collective_id=0, has_side_effects=True),
-    )(share)
-
-
 def head_norm_rope(values, gain, cosine, sine):
     lane = lax.broadcasted_iota(jnp.int32, (values.shape[0], 128), 1)
     low = lane < HEAD
@@ -212,10 +151,9 @@
 
         centred = part - average(part)
         unit = centred * lax.rsqrt(average(centred * centred) + 1e-06)
-        unit = unit * gain[:, g * 128 : (g + 1) * 128]
+        unit = unit * gain
         turned = jnp.where(lane % 2 == 0, pltpu.roll(unit, 127, 1), pltpu.roll(unit, 1, 1))
-        cos_part = cosine[:, g * 128 : (g + 1) * 128]
-        groups.append(unit * cos_part + turned * sine[:, g * 128 : (g + 1) * 128])
+        groups.append(unit * cosine + turned * sine)
     return jnp.concatenate(groups, axis=1)
 
 
@@ -228,8 +166,7 @@
     gain_ref,
     cos_ref,
     sin_ref,
-    video_ref,
-    limit_ref,
+    length_ref,
     out_ref,
     kv_ref,
     w_qkv,
@@ -239,6 +176,8 @@
     fresh_all,
     partial,
     reduced,
+    mod_all,
+    mod_tiles,
     w_sems,
     x_send,
     x_recv,
@@ -249,6 +188,11 @@
     stale_recv,
     fresh_send,
     fresh_recv,
+    mod_local,
+    mod_tp_send,
+    mod_tp_recv,
+    mod_send,
+    mod_recv,
 ):
     x, z, c = place()
     tp = lax.axis_index("tp")
@@ -263,24 +207,51 @@
     across = [{"section": 1 - section, "tp": (tp + d) % 4} for d in (0,) + OTHERS]
     greet(tp_peers() + seq_peers() + across)
 
+    own_mod = mod_all.at[x, z, c]
+    keep = pltpu.make_async_copy(mod_ref, own_mod.at[tp], mod_local)
+    keep.start()
+
+    def mod_copy(k, source):
+        return remote(
+            mod_ref, own_mod.at[source], mod_tp_send.at[k], mod_tp_recv.at[source], tp_peers()[k]
+        )
+
+    for k in range(3):
+        mod_copy(k, tp).start()
+
     @pl.when(section == 0)
     def _():
         for k, peer in enumerate(tp_peers()):
             remote(hidden_ref, x_all.at[tp], x_send.at[k], x_recv.at[tp], peer).start()
         x_all[tp] = hidden_ref[...]
 
+    keep.wait()
+    for k, d in enumerate(OTHERS):
+        mod_copy(k, (tp + d) % 4).wait_recv()
     stale = SeqGather(stale_ref, stale_all, stale_send, stale_recv)
-    stale.start()
+    modulation = SeqGather(own_mod, mod_all, mod_send, mod_recv)
+    modulation.start()
+    stale.start_z()
     stale_all[x, z, c] = stale_ref[...]
+    modulation.forward_z()
+    stale.start_x()
 
     def x_arrived(source):
         remote(
             hidden_ref, x_all.at[source], x_send.at[0], x_recv.at[source], tp_peers()[0]
         ).wait_recv()
 
+    modulation.forward_x()
+    modulation.finish()
+    groups = mod_all[...].reshape(16, 8, 2, 128)
+    blank = jnp.zeros((16, 1, 128), jnp.float32)
+    mod_tiles[...] = jnp.concatenate([groups[:, :, 0], blank], axis=1) + jnp.concatenate(
+        [blank, groups[:, :, 1]], axis=1
+    )
+    stale.forward_z()
+
     @pl.when(section == 1)
     def _():
-        stale.forward_z()
         stale.forward_x()
         stale.finish()
         x_arrived(tp)
@@ -288,8 +259,22 @@
     for d in OTHERS:
         x_arrived((tp + d) % 4)
 
-    video = video_ref[...] > 0.0
+    token = lax.axis_index("seq") * rows + lax.broadcasted_iota(jnp.int32, (rows, 1), 0)
+    video = token >= TEXT
     width = share * 4
+    tiles = share // 128
+
+    def mod_tile(row, index):
+        tile = row * (width // 128) + index
+        return mod_tiles[tile // 9, tile % 9 : tile % 9 + 1, :]
+
+    def mod_rows(row, t):
+        parts = [
+            jnp.where(video, mod_tile(row, t * tiles + i), mod_tile(row + 3, t * tiles + i))
+            for i in range(tiles)
+        ]
+        return jnp.concatenate(parts, axis=1)
+
     total = jnp.zeros((rows, 1), jnp.float32)
     for t in range(4):
         total += jnp.sum(x_all[t].astype(jnp.float32), axis=1, keepdims=True)
@@ -299,23 +284,19 @@
         centred = x_all[t].astype(jnp.float32) - mean
         square += jnp.sum(centred * centred, axis=1, keepdims=True)
     inverse = lax.rsqrt(square * (1.0 / width) + 1e-05)
-
-    @pl.when(section == 0)
-    def _():
-        stale.forward_z()
-
     load_qkv.wait()
     proj = [jnp.zeros((rows, head_cols), jnp.float32) for _ in range(3)]
     for t in range(4):
         cols = slice(t * share, (t + 1) * share)
-        shift = jnp.where(video, mod_ref[0:1, cols], mod_ref[3:4, cols])
-        scale = jnp.where(video, mod_ref[1:2, cols], mod_ref[4:5, cols])
+        shift = mod_rows(0, t)
+        scale = mod_rows(1, t)
         centred = x_all[t].astype(jnp.float32) - mean
         normed = (centred * inverse * (1.0 + scale) + shift).astype(jnp.bfloat16)
         for part in (1, 2, 0):
             proj[part] += jnp.dot(normed, w_qkv[part, cols, :], preferred_element_type=jnp.float32)
     cosine, sine = cos_ref[...], sin_ref[...]
-    keys = head_norm_rope(proj[1], gain_ref[1:2, :], cosine, sine).astype(jnp.bfloat16)
+    gains = jnp.concatenate([gain_ref[...]] * 2, axis=1)
+    keys = head_norm_rope(proj[1], gains[1:2], cosine, sine).astype(jnp.bfloat16)
     kv_ref[0] = keys
     kv_ref[1] = proj[2].astype(jnp.bfloat16)
     fresh_all[x, z, c, 0] = keys
@@ -327,7 +308,7 @@
     def _():
         stale.forward_x()
 
-    queries = head_norm_rope(proj[0], gain_ref[0:1, :], cosine, sine)
+    queries = head_norm_rope(proj[0], gains[0:1], cosine, sine)
     stacked = jnp.concatenate([queries] * heads, axis=0)
     row_head = lax.broadcasted_iota(jnp.int32, stacked.shape, 0) // rows
     col_head = lax.broadcasted_iota(jnp.int32, stacked.shape, 1) // HEAD
@@ -353,7 +334,12 @@
         spread, all_rows(fresh_all, 0), contract, preferred_element_type=jnp.float32
     )
     column = lax.broadcasted_iota(jnp.int32, scores_fresh.shape, 1)
-    allowed = column < limit_ref[...]
+    first = TEXT + length_ref[0]
+    second = first + length_ref[1]
+    third = second + length_ref[2]
+    limit = jnp.where(token < third, third, tokens)
+    limit = jnp.where(token < first, first, jnp.where(token < second, second, limit))
+    allowed = column < jnp.concatenate([limit] * heads, axis=0)
     scores = jnp.where(allowed, scores_fresh, scores_stale) * HEAD ** (-0.5)
     weights = jnp.exp(scores - jnp.max(scores, axis=1, keepdims=True))
     denominator = jnp.sum(weights, axis=1, keepdims=True)
@@ -380,8 +366,9 @@
         )
         copy.start()
         r_copies.append(copy)
-    mine = pl.ds(pl.multiple_of(tp * share, 128), share)
-    gate = jnp.where(video, mod_ref[2:3, mine], mod_ref[5:6, mine])
+    gate = jnp.zeros((rows, share), jnp.float32)
+    for t in range(4):
+        gate = jnp.where(tp == t, mod_rows(2, t), gate)
     projected = partial[tp].astype(jnp.float32)
     for k, d in enumerate(OTHERS):
         source = (tp + d) % 4
@@ -405,11 +392,14 @@
 
     for copy in r_copies:
         copy.wait_send()
+    for k in range(3):
+        mod_copy(k, tp).wait_send()
+    modulation.drain()
     stale.drain()
     fresh.drain()
 
 
-def run_layers(hidden, w_qkv, w_out, stale, modulate, gains, cosine, sine, video, limits):
+def run_layers(hidden, w_qkv, w_out, stale, modulate, gains, cosine, sine, lengths):
     rows, share = hidden.shape
     head_cols = w_out.shape[0]
     blocks = pltpu.VMEM((4, 4, 2, 2, rows, head_cols), jnp.bfloat16)
@@ -421,7 +411,9 @@
             jax.ShapeDtypeStruct((rows, share), jnp.bfloat16),
             jax.ShapeDtypeStruct((2, rows, head_cols), jnp.bfloat16),
         ),
-        in_specs=[VMEM_SPEC, any_spec, any_spec] + [VMEM_SPEC] * 7,
+        in_specs=[VMEM_SPEC, any_spec, any_spec]
+        + [VMEM_SPEC] * 5
+        + [pl.BlockSpec(memory_space=pltpu.SMEM)],
         out_specs=(VMEM_SPEC, VMEM_SPEC),
         scratch_shapes=[
             pltpu.VMEM(w_qkv.shape, jnp.bfloat16),
@@ -431,6 +423,8 @@
             blocks,
             pltpu.VMEM((4, rows, share), jnp.bfloat16),
             pltpu.VMEM((4, rows, share), jnp.bfloat16),
+            pltpu.VMEM((4, 4, 2, 4, 2, 128), jnp.float32),
+            pltpu.VMEM((16, 9, 128), jnp.float32),
             dma((2,)),
             dma((3,)),
             dma((4,)),
@@ -441,9 +435,31 @@
             dma((4, 4, 2)),
             dma((GATHER_SENDS,)),
             dma((4, 4, 2)),
+            dma,
+            dma((3,)),
+            dma((4,)),
+            dma((GATHER_SENDS,)),
+            dma((4, 4, 2)),
         ],
-        compiler_params=pltpu.CompilerParams(collective_id=1, has_side_effects=True),
-    )(hidden, w_qkv, w_out, stale, modulate, gains, cosine, sine, video, limits)
+        compiler_params=pltpu.CompilerParams(collective_id=0, has_side_effects=True),
+    )(hidden, w_qkv, w_out, stale, modulate, gains, cosine, sine, lengths)
+
+
+def rope_tables(positions, first_row):
+    column = jnp.arange(128)
+    pair = (column % HEAD) // 2
+    spans = ((0, HEAD // 4), (HEAD // 8, 3 * HEAD // 8), (5 * HEAD // 16, 3 * HEAD // 8))
+    coords = positions.astype(jnp.float32)
+    angles = jnp.zeros((positions.shape[1], 128), jnp.float32)
+    for axis, (start, size) in enumerate(spans):
+        exponent = 2.0 * (pair - start).astype(jnp.float32) / size
+        inside = (pair >= start) & (pair < start + size // 2)
+        frequency = jnp.where(inside, 1.0 / 10000.0**exponent, 0.0)
+        angles = angles + coords[axis][:, None] * frequency[None, :]
+    video = (first_row + jnp.arange(positions.shape[1]) >= TEXT)[:, None]
+    sign = jnp.where(column % 2 == 0, -1.0, 1.0)[None, :]
+    cosine = jnp.where(video, jnp.cos(angles), 1.0)
+    return cosine, jnp.where(video, jnp.sin(angles) * sign, 0.0)
 
 
 def local(
@@ -458,33 +474,22 @@
     timestep,
 ):
     tok_rows = hidden.shape[0]
-    head_count = qkv_weight.shape[3] // HEAD
     seq_rank = lax.axis_index("seq")
     share = jnp.dot(time_features(timestep), mod_weight[0], preferred_element_type=jnp.float32)
-    modulate = gather_modulation(share).reshape(6, -1)
-    my_rows = seq_rank * tok_rows + jnp.arange(tok_rows, dtype=jnp.int32)
-    video = (my_rows >= TEXT)[:, None]
-    bounds = jnp.cumsum(patch_lengths)
-    query_patch = patch_index(my_rows, bounds)
-    ends = jnp.where(jnp.arange(bounds.shape[0]) == bounds.shape[0] - 1, 1 << 30, TEXT + bounds)
-    is_patch = query_patch[:, None] == jnp.arange(bounds.shape[0])[None, :]
-    limits = jnp.sum(jnp.where(is_patch, ends[None, :], 0), axis=1, keepdims=True)
-    limits = jnp.tile(limits.astype(jnp.int32), (head_count, 1))
-    cosine, sine = rope_tables(positions, head_count)
-    even = jnp.arange(cosine.shape[1]) % 2 == 0
-    cosine = jnp.where(video, cosine, 1.0)
-    sine = jnp.where(video, jnp.where(even, -sine, sine), 0.0)
+    device = seq_rank * lax.axis_size("tp") + lax.axis_index("tp")
+    offset = (share.shape[1] * device) % 128
+    placed = lax.dynamic_update_slice(jnp.zeros((1, 256), jnp.float32), share, (0, offset))
+    cosine, sine = rope_tables(positions, seq_rank * tok_rows)
     result, fresh_kv = run_layers(
         hidden,
         jnp.transpose(qkv_weight[0], (1, 0, 2)),
         out_weight[0],
         stale_kv[0],
-        modulate,
-        jnp.tile(qk_gain[0], (1, head_count)),
+        placed.reshape(2, 128),
+        qk_gain[0],
         cosine,
         sine,
-        video.astype(jnp.float32),
-        limits,
+        patch_lengths,
     )
     return (result[None], fresh_kv[None])
 

time: 99.2 us -> 83.4 us (0.84)
  Pallas kernels: 85.5 us -> 76.5 us
  local copies, waits for them, and re-layouts: 6.27 us -> 3.05 us
  other arithmetic: 4.6 us -> 1.55 us
    pallas_call x1 -> x0, Pallas kernels: 21.7 us -> none  [gather_modulation(): pl.pallas_call(modulation_kernel, out_shape=jax.ShapeDtypeStruct((4, 4, 2...]
    pallas_call x1, Pallas kernels: 63.8 us -> 76.5 us  [run_layers(): pl.pallas_call(layer_kernel, out_shape=(jax.ShapeDtypeStruct((rows, share...]
    another operation x8 -> x0, local copies, waits for them, and re-layouts: 2.3 us -> none  [the longest x2 1.35 us: local(): jnp.tile(qk_gain[0], (1, head_count))]
    pallas_call x1 -> x0, other arithmetic: 1.25 us -> none  [gather_modulation(): pl.pallas_call(modulation_kernel, out_shape=jax.ShapeDtypeStruct((4, 4, 2...]
    unnamed x4 -> x6, local copies, waits for them, and re-layouts: 3 us -> 2.93 us
where the time goes in v3:
time: 83.4 us; the launch traced here: 82.6 us
  Pallas kernels  76.5 us (92%)
  local copies, waits for them, and re-layouts  3.05 us (4%)
  other arithmetic  1.55 us (2%)
  between operations  1.4 us (2%)
    pallas_call x1, Pallas kernels, run_layers(): pl.pallas_call(layer_kernel, out_shape=(jax.ShapeDtypeStruct((rows, share...  76.5 us
    unnamed x6, local copies, waits for them, and re-layouts  2.93 us

profile of v3, /device:TPU:32, one launch (start us, length us, event | category | flops | bytes accessed | tf_op | source)
XLA Modules:
  0.0 82.6 jit_solution(5682362109755726945)
XLA Ops:
  0.6 0.0 copy-start
  1.5 0.1 copy-done
  1.6 0.1 fusion
  1.7 0.1 dynamic_update_slice.3
  1.8 0.0 copy-start.1
  1.8 0.7 convert_element_type.45
  2.5 0.8 multiply_select_fusion
  3.3 0.0 copy-done.1
  3.3 76.5 %shard_map.104 = (bf16[32,768]{1,0:T(8,128)(2,1)}, bf16[2,32,384]{2,1,0:T(8,128)(2,1)}) custom-call(bf16[32,768]{1,0:T(8,128)(2,1)} %hidden_ref.1, bf16[3,3072,384]{2,1,0:T(8,128)(2,1)} %bitcast.21, bf16[384,3072]{1,0:T(8,128)(2,1)} %bitcast.22, bf16[2,32,384]{2,1,0:T(8,128)(2,1)} %bitcast.23, f32[2,128]{1,0:T(2,128)} %bitcast.27, f32[2,64]{1,0:T(2,128)} %bitcast.26, ...), custom_call_target="tpu_custom_call" | custom-call | tf_op jit(solution)/shard_map/pallas_call | solution.py:408
  79.7 1.4 %copy.15 = bf16[1,32,768]{2,1,0:T(8,128)(2,1)} copy(bf16[1,32,768]{2,1,0:T(8,128)(2,1)} %bitcast.25) | data formatting | bytes 98304
  81.2 1.4 %copy.16 = bf16[1,2,32,384]{3,2,1,0:T(8,128)(2,1)} copy(bf16[1,2,32,384]{3,2,1,0:T(8,128)(2,1)} %bitcast.24) | data formatting | bytes 98304
  (8 shorter events, 0.1 us)
Async XLA Ops:
  0.6 0.9 %copy-start = (bf16[1,512,144]{1,2,0:T(8,128)(2,1)S(1)}, bf16[1,512,144]{1,2,0:T(8,128)(2,1)}, u32[]{:S(2)}) copy-start(bf16[1,512,144]{1,2,0:T(8,128)(2,1)} %param.13) | copy-start | bytes 442372
  1.8 1.5 %copy-start.1 = (f32[1,256]{1,0:T(1,128)}, f32[1,256]{1,0:T(1,128)S(1)}, u32[]{:S(2)}) copy-start(f32[1,256]{1,0:T(1,128)S(1)} %dynamic_update_slice.3) | copy-start | bytes 3076

commit v4 on v3

--- a/solution.py
+++ b/solution.py
@@ -57,6 +57,19 @@
 def tp_peers():
     tp = lax.axis_index("tp")
     return [{"tp": (tp + d) % 4} for d in OTHERS]
+
+
+def chip_column_peers():
+    x, z, c = place()
+    pairs = [(dz, dc) for dz in (0,) + OTHERS for dc in (0, 1) if (dz, dc) != (0, 0)]
+    return [{"seq": seq_of(x, (z + dz) % 4, (c + dc) % 2)} for dz, dc in pairs]
+
+
+def plane_peers():
+    x, z, c = place()
+    tp = lax.axis_index("tp")
+    pairs = [(dx, dt) for dx in (0,) + OTHERS for dt in (0,) + OTHERS if (dx, dt) != (0, 0)]
+    return [{"seq": seq_of((x + dx) % 4, z, c), "tp": (tp + dt) % 4} for dx, dt in pairs]
 
 
 def greet(peers):
@@ -173,11 +186,11 @@
     w_out,
     x_all,
     stale_all,
-    fresh_all,
+    fresh_keys,
+    fresh_values,
     partial,
     reduced,
     mod_all,
-    mod_tiles,
     w_sems,
     x_send,
     x_recv,
@@ -186,13 +199,14 @@
     r_recv,
     stale_send,
     stale_recv,
-    fresh_send,
-    fresh_recv,
+    key_send,
+    key_recv,
+    value_send,
+    value_recv,
     mod_local,
-    mod_tp_send,
-    mod_tp_recv,
     mod_send,
-    mod_recv,
+    column_recv,
+    plane_recv,
 ):
     x, z, c = place()
     tp = lax.axis_index("tp")
@@ -205,19 +219,7 @@
     load_qkv.start()
     load_out.start()
     across = [{"section": 1 - section, "tp": (tp + d) % 4} for d in (0,) + OTHERS]
-    greet(tp_peers() + seq_peers() + across)
-
-    own_mod = mod_all.at[x, z, c]
-    keep = pltpu.make_async_copy(mod_ref, own_mod.at[tp], mod_local)
-    keep.start()
-
-    def mod_copy(k, source):
-        return remote(
-            mod_ref, own_mod.at[source], mod_tp_send.at[k], mod_tp_recv.at[source], tp_peers()[k]
-        )
-
-    for k in range(3):
-        mod_copy(k, tp).start()
+    greet(chip_column_peers() + plane_peers() + across)
 
     @pl.when(section == 0)
     def _():
@@ -225,29 +227,57 @@
             remote(hidden_ref, x_all.at[tp], x_send.at[k], x_recv.at[tp], peer).start()
         x_all[tp] = hidden_ref[...]
 
+    keep = pltpu.make_async_copy(mod_ref, mod_all.at[x, tp, z, c], mod_local)
+    keep.start()
+
+    def column_copy(k, from_z, from_c):
+        return remote(
+            mod_ref,
+            mod_all.at[x, tp, from_z, from_c],
+            mod_send.at[k],
+            column_recv.at[from_z, from_c],
+            chip_column_peers()[k],
+        )
+
+    def plane_copy(k, from_x, from_tp):
+        return remote(
+            mod_all.at[from_x, from_tp],
+            mod_all.at[from_x, from_tp],
+            mod_send.at[7 + k],
+            plane_recv.at[from_x, from_tp],
+            plane_peers()[k],
+        )
+
+    for k in range(7):
+        column_copy(k, z, c).start()
+    stale = SeqGather(stale_ref, stale_all, stale_send, stale_recv)
+
+    @pl.when(section == 0)
+    def _():
+        stale.start()
+
+    stale_all[x, z, c] = stale_ref[...]
     keep.wait()
-    for k, d in enumerate(OTHERS):
-        mod_copy(k, (tp + d) % 4).wait_recv()
-    stale = SeqGather(stale_ref, stale_all, stale_send, stale_recv)
-    modulation = SeqGather(own_mod, mod_all, mod_send, mod_recv)
-    modulation.start()
-    stale.start_z()
-    stale_all[x, z, c] = stale_ref[...]
-    modulation.forward_z()
-    stale.start_x()
+    for dz in (0,) + OTHERS:
+        for dc in (0, 1):
+            if (dz, dc) != (0, 0):
+                column_copy(0, (z + dz) % 4, (c + dc) % 2).wait_recv()
+    for k in range(15):
+        plane_copy(k, x, tp).start()
+    for dx in (0,) + OTHERS:
+        for dt in (0,) + OTHERS:
+            if (dx, dt) != (0, 0):
+                plane_copy(0, (x + dx) % 4, (tp + dt) % 4).wait_recv()
 
     def x_arrived(source):
         remote(
             hidden_ref, x_all.at[source], x_send.at[0], x_recv.at[source], tp_peers()[0]
         ).wait_recv()
 
-    modulation.forward_x()
-    modulation.finish()
-    groups = mod_all[...].reshape(16, 8, 2, 128)
-    blank = jnp.zeros((16, 1, 128), jnp.float32)
-    mod_tiles[...] = jnp.concatenate([groups[:, :, 0], blank], axis=1) + jnp.concatenate(
-        [blank, groups[:, :, 1]], axis=1
-    )
+    @pl.when(section == 1)
+    def _():
+        stale.start()
+
     stale.forward_z()
 
     @pl.when(section == 1)
@@ -265,8 +295,13 @@
     tiles = share // 128
 
     def mod_tile(row, index):
-        tile = row * (width // 128) + index
-        return mod_tiles[tile // 9, tile % 9 : tile % 9 + 1, :]
+        group, step = divmod(row * (width // 128) + index, 9)
+        found = None
+        for member, half in ((step, 0), (step - 1, 1)):
+            if 0 <= member < 8:
+                at = (group // 4, member % 4, group % 4, member // 4, slice(half, half + 1))
+                found = mod_all[at] if found is None else found + mod_all[at]
+        return found
 
     def mod_rows(row, t):
         parts = [
@@ -285,35 +320,43 @@
         square += jnp.sum(centred * centred, axis=1, keepdims=True)
     inverse = lax.rsqrt(square * (1.0 / width) + 1e-05)
     load_qkv.wait()
-    proj = [jnp.zeros((rows, head_cols), jnp.float32) for _ in range(3)]
+    normed = []
     for t in range(4):
-        cols = slice(t * share, (t + 1) * share)
-        shift = mod_rows(0, t)
-        scale = mod_rows(1, t)
         centred = x_all[t].astype(jnp.float32) - mean
-        normed = (centred * inverse * (1.0 + scale) + shift).astype(jnp.bfloat16)
-        for part in (1, 2, 0):
-            proj[part] += jnp.dot(normed, w_qkv[part, cols, :], preferred_element_type=jnp.float32)
+        scaled = centred * inverse * (1.0 + mod_rows(1, t)) + mod_rows(0, t)
+        normed.append(scaled.astype(jnp.bfloat16))
+
+    def project(part):
+        proj = jnp.zeros((rows, head_cols), jnp.float32)
+        for t in range(4):
+            weights = w_qkv[part, t * share : (t + 1) * share, :]
+            proj += jnp.dot(normed[t], weights, preferred_element_type=jnp.float32)
+        return proj
+
     cosine, sine = cos_ref[...], sin_ref[...]
     gains = jnp.concatenate([gain_ref[...]] * 2, axis=1)
-    keys = head_norm_rope(proj[1], gains[1:2], cosine, sine).astype(jnp.bfloat16)
+    keys = head_norm_rope(project(1), gains[1:2], cosine, sine).astype(jnp.bfloat16)
     kv_ref[0] = keys
-    kv_ref[1] = proj[2].astype(jnp.bfloat16)
-    fresh_all[x, z, c, 0] = keys
-    fresh_all[x, z, c, 1] = proj[2].astype(jnp.bfloat16)
-    fresh = SeqGather(kv_ref, fresh_all, fresh_send, fresh_recv)
-    fresh.start()
+    fresh_keys[x, z, c] = keys
+    key_gather = SeqGather(kv_ref.at[0], fresh_keys, key_send, key_recv)
+    key_gather.start()
+    values = project(2).astype(jnp.bfloat16)
+    kv_ref[1] = values
+    fresh_values[x, z, c] = values
+    value_gather = SeqGather(kv_ref.at[1], fresh_values, value_send, value_recv)
+    value_gather.start()
 
     @pl.when(section == 0)
     def _():
         stale.forward_x()
 
-    queries = head_norm_rope(proj[0], gains[0:1], cosine, sine)
+    queries = head_norm_rope(project(0), gains[0:1], cosine, sine)
     stacked = jnp.concatenate([queries] * heads, axis=0)
     row_head = lax.broadcasted_iota(jnp.int32, stacked.shape, 0) // rows
     col_head = lax.broadcasted_iota(jnp.int32, stacked.shape, 1) // HEAD
     spread = jnp.where(row_head == col_head, stacked, 0.0).astype(jnp.bfloat16)
-    fresh.forward_z()
+    key_gather.forward_z()
+    value_gather.forward_z()
 
     @pl.when(section == 0)
     def _():
@@ -321,17 +364,17 @@
 
     tokens = rows * 32
 
-    def all_rows(blocks, which):
-        return blocks[:, :, :, which].reshape(tokens, head_cols)
+    def all_rows(blocks):
+        return blocks.reshape(tokens, head_cols)
 
     contract = (((1,), (1,)), ((), ()))
     scores_stale = lax.dot_general(
-        spread, all_rows(stale_all, 0), contract, preferred_element_type=jnp.float32
-    )
-    fresh.forward_x()
-    fresh.finish()
+        spread, all_rows(stale_all[:, :, :, 0]), contract, preferred_element_type=jnp.float32
+    )
+    key_gather.forward_x()
+    key_gather.finish()
     scores_fresh = lax.dot_general(
-        spread, all_rows(fresh_all, 0), contract, preferred_element_type=jnp.float32
+        spread, all_rows(fresh_keys[...]), contract, preferred_element_type=jnp.float32
     )
     column = lax.broadcasted_iota(jnp.int32, scores_fresh.shape, 1)
     first = TEXT + length_ref[0]
@@ -345,8 +388,12 @@
     denominator = jnp.sum(weights, axis=1, keepdims=True)
     part_fresh = jnp.where(allowed, weights, 0.0).astype(jnp.bfloat16)
     part_stale = jnp.where(allowed, 0.0, weights).astype(jnp.bfloat16)
-    mixed = jnp.dot(part_fresh, all_rows(fresh_all, 1), preferred_element_type=jnp.float32)
-    mixed += jnp.dot(part_stale, all_rows(stale_all, 1), preferred_element_type=jnp.float32)
+    mixed = jnp.dot(
+        part_stale, all_rows(stale_all[:, :, :, 1]), preferred_element_type=jnp.float32
+    )
+    value_gather.forward_x()
+    value_gather.finish()
+    mixed += jnp.dot(part_fresh, all_rows(fresh_values[...]), preferred_element_type=jnp.float32)
     mixed = jnp.where(row_head == col_head, mixed / denominator, 0.0)
     attended = mixed[0:rows]
     for h in range(1, heads):
@@ -392,17 +439,20 @@
 
     for copy in r_copies:
         copy.wait_send()
-    for k in range(3):
-        mod_copy(k, tp).wait_send()
-    modulation.drain()
+    for k in range(7):
+        column_copy(k, z, c).wait_send()
+    for k in range(15):
+        plane_copy(k, x, tp).wait_send()
     stale.drain()
-    fresh.drain()
+    key_gather.drain()
+    value_gather.drain()
 
 
 def run_layers(hidden, w_qkv, w_out, stale, modulate, gains, cosine, sine, lengths):
     rows, share = hidden.shape
     head_cols = w_out.shape[0]
     blocks = pltpu.VMEM((4, 4, 2, 2, rows, head_cols), jnp.bfloat16)
+    half_blocks = pltpu.VMEM((4, 4, 2, rows, head_cols), jnp.bfloat16)
     dma = pltpu.SemaphoreType.DMA
     any_spec = pl.BlockSpec(memory_space=pl.ANY)
     return pl.pallas_call(
@@ -420,11 +470,11 @@
             pltpu.VMEM(w_out.shape, jnp.bfloat16),
             pltpu.VMEM((4, rows, share), jnp.bfloat16),
             blocks,
-            blocks,
+            half_blocks,
+            half_blocks,
             pltpu.VMEM((4, rows, share), jnp.bfloat16),
             pltpu.VMEM((4, rows, share), jnp.bfloat16),
-            pltpu.VMEM((4, 4, 2, 4, 2, 128), jnp.float32),
-            pltpu.VMEM((16, 9, 128), jnp.float32),
+            pltpu.VMEM((4, 4, 4, 2, 2, 128), jnp.float32),
             dma((2,)),
             dma((3,)),
             dma((4,)),
@@ -435,11 +485,12 @@
             dma((4, 4, 2)),
             dma((GATHER_SENDS,)),
             dma((4, 4, 2)),
-            dma,
-            dma((3,)),
-            dma((4,)),
             dma((GATHER_SENDS,)),
             dma((4, 4, 2)),
+            dma,
+            dma((22,)),
+            dma((4, 2)),
+            dma((4, 4)),
         ],
         compiler_params=pltpu.CompilerParams(collective_id=0, has_side_effects=True),
     )(hidden, w_qkv, w_out, stale, modulate, gains, cosine, sine, lengths)

time: 83.4 us -> 78.3 us (0.939)
  Pallas kernels: 76.5 us -> 71.9 us
    pallas_call x1, Pallas kernels: 76.5 us -> 71.9 us  [run_layers(): pl.pallas_call(layer_kernel, out_shape=(jax.ShapeDtypeStruct((rows, share...]
where the time goes in v4:
time: 78.3 us; the launch traced here: 78 us
  Pallas kernels  71.9 us (92%)
  local copies, waits for them, and re-layouts  3.05 us (4%)
  other arithmetic  1.55 us (2%)
  between operations  1.4 us (2%)
    pallas_call x1, Pallas kernels, run_layers(): pl.pallas_call(layer_kernel, out_shape=(jax.ShapeDtypeStruct((rows, share...  71.9 us
    unnamed x6, local copies, waits for them, and re-layouts  2.93 us

profile of v4, /device:TPU:32, one launch (start us, length us, event | category | flops | bytes accessed | tf_op | source)
XLA Modules:
  0.0 78.0 jit_solution(4213826070061481358)
XLA Ops:
  0.6 0.0 copy-start
  1.5 0.1 copy-done
  1.6 0.1 fusion
  1.7 0.1 dynamic_update_slice.3
  1.8 0.0 copy-start.1
  1.8 0.7 convert_element_type.45
  2.5 0.8 multiply_select_fusion
  3.3 0.0 copy-done.1
  3.3 71.9 %shard_map.104 = (bf16[32,768]{1,0:T(8,128)(2,1)}, bf16[2,32,384]{2,1,0:T(8,128)(2,1)}) custom-call(bf16[32,768]{1,0:T(8,128)(2,1)} %hidden_ref.1, bf16[3,3072,384]{2,1,0:T(8,128)(2,1)} %bitcast.21, bf16[384,3072]{1,0:T(8,128)(2,1)} %bitcast.22, bf16[2,32,384]{2,1,0:T(8,128)(2,1)} %bitcast.23, f32[2,128]{1,0:T(2,128)} %bitcast.27, f32[2,64]{1,0:T(2,128)} %bitcast.26, ...), custom_call_target="tpu_custom_call" | custom-call | tf_op jit(solution)/shard_map/pallas_call | solution.py:458
  75.1 1.4 %copy.15 = bf16[1,32,768]{2,1,0:T(8,128)(2,1)} copy(bf16[1,32,768]{2,1,0:T(8,128)(2,1)} %bitcast.25) | data formatting | bytes 98304
  76.6 1.4 %copy.16 = bf16[1,2,32,384]{3,2,1,0:T(8,128)(2,1)} copy(bf16[1,2,32,384]{3,2,1,0:T(8,128)(2,1)} %bitcast.24) | data formatting | bytes 98304
  (8 shorter events, 0.1 us)
Async XLA Ops:
  0.6 0.9 %copy-start = (bf16[1,512,144]{1,2,0:T(8,128)(2,1)S(1)}, bf16[1,512,144]{1,2,0:T(8,128)(2,1)}, u32[]{:S(2)}) copy-start(bf16[1,512,144]{1,2,0:T(8,128)(2,1)} %param.13) | copy-start | bytes 442372
  1.8 1.5 %copy-start.1 = (f32[1,256]{1,0:T(1,128)}, f32[1,256]{1,0:T(1,128)S(1)}, u32[]{:S(2)}) copy-start(f32[1,256]{1,0:T(1,128)S(1)} %dynamic_update_slice.3) | copy-start | bytes 3076

commit v5 on v4

--- a/solution.py
+++ b/solution.py
@@ -79,6 +79,11 @@
     pl.semaphore_wait(barrier, len(peers))
 
 
+def relay_order():
+    c = lax.axis_index("seq") % 2
+    return (3 - 2 * c, 1 + 2 * c, 2)
+
+
 class SeqGather:
     def __init__(self, own, blocks, send_sems, recv_sems):
         self.own, self.blocks = own, blocks
@@ -99,38 +104,43 @@
             block, block, self.send_sems.at[0], self.recv_sems.at[x, z, c], seq_peers()[-1]
         ).wait_recv()
 
-    def start_z(self):
+    def start(self):
         x, z, c = place()
-        for k, peer in enumerate(seq_peers()[:3]):
+        peers = seq_peers()
+        for k, peer in enumerate(peers[:2] + peers[3:5] + peers[-1:]):
             self.send(k, self.own, x, z, c, peer)
-
-    def start_x(self):
-        x, z, c = place()
-        for k, peer in enumerate(seq_peers()[3:]):
-            self.send(3 + k, self.own, x, z, c, peer)
-
-    def start(self):
-        self.start_z()
-        self.start_x()
 
     def forward_z(self):
         x, z, c = place()
         peers = seq_peers()
-        for i, d in enumerate(OTHERS):
+        slot = 5
+        for i, d in enumerate(relay_order()):
             from_z = (z + d) % 4
+            block = self.blocks.at[x, from_z, c]
             self.arrived(x, from_z, c)
-            for k, peer in enumerate(peers[3:]):
-                self.send(7 + 4 * i + k, self.blocks.at[x, from_z, c], x, from_z, c, peer)
+            onward = [{"seq": seq_of(x, (z + 4 - d) % 4, c)}] if i == 0 else []
+            for peer in onward + peers[3:5] + peers[-1:]:
+                self.send(slot, block, x, from_z, c, peer)
+                slot += 1
+
+    def pass_x(self, i, d, slot):
+        x, z, c = place()
+        from_x = (x + d) % 4
+        for dz in (0,) + relay_order():
+            from_z = (z + dz) % 4
+            block = self.blocks.at[from_x, from_z, c]
+            self.arrived(from_x, from_z, c)
+            onward = [{"seq": seq_of((x + 4 - d) % 4, z, c)}] if i == 0 else []
+            for peer in onward + seq_peers()[-1:]:
+                self.send(slot, block, from_x, from_z, c, peer)
+                slot += 1
+
+    def relay_x(self):
+        self.pass_x(0, relay_order()[0], 15)
 
     def forward_x(self):
-        x, z, c = place()
-        partner = seq_peers()[-1]
-        for i, dz in enumerate((0,) + OTHERS):
-            for k, dx in enumerate(OTHERS):
-                from_x, from_z = (x + dx) % 4, (z + dz) % 4
-                self.arrived(from_x, from_z, c)
-                block = self.blocks.at[from_x, from_z, c]
-                self.send(19 + 3 * i + k, block, from_x, from_z, c, partner)
+        self.pass_x(1, relay_order()[1], 23)
+        self.pass_x(2, relay_order()[2], 27)
 
     def finish(self):
         x, z, c = place()
@@ -147,7 +157,7 @@
             ).wait_send()
 
 
-GATHER_SENDS = 7 + 12 + 12
+GATHER_SENDS = 5 + 10 + 16
 
 
 def head_norm_rope(values, gain, cosine, sine):
@@ -282,6 +292,7 @@
 
     @pl.when(section == 1)
     def _():
+        stale.relay_x()
         stale.forward_x()
         stale.finish()
         x_arrived(tp)
@@ -346,21 +357,25 @@
     value_gather = SeqGather(kv_ref.at[1], fresh_values, value_send, value_recv)
     value_gather.start()
 
-    @pl.when(section == 0)
-    def _():
-        stale.forward_x()
-
     queries = head_norm_rope(project(0), gains[0:1], cosine, sine)
     stacked = jnp.concatenate([queries] * heads, axis=0)
     row_head = lax.broadcasted_iota(jnp.int32, stacked.shape, 0) // rows
     col_head = lax.broadcasted_iota(jnp.int32, stacked.shape, 1) // HEAD
     spread = jnp.where(row_head == col_head, stacked, 0.0).astype(jnp.bfloat16)
+
+    @pl.when(section == 0)
+    def _():
+        stale.relay_x()
+
     key_gather.forward_z()
     value_gather.forward_z()
 
     @pl.when(section == 0)
     def _():
+        stale.forward_x()
         stale.finish()
+
+    key_gather.relay_x()
 
     tokens = rows * 32
 
@@ -373,6 +388,7 @@
     )
     key_gather.forward_x()
     key_gather.finish()
+    value_gather.relay_x()
     scores_fresh = lax.dot_general(
         spread, all_rows(fresh_keys[...]), contract, preferred_element_type=jnp.float32
     )

time: 78.3 us -> 94.7 us (1.21)
  Pallas kernels: 71.9 us -> 88.3 us
    pallas_call x1, Pallas kernels: 71.9 us -> 88.3 us  [run_layers(): pl.pallas_call(layer_kernel, out_shape=(jax.ShapeDtypeStruct((rows, share...]
where the time goes in v5:
time: 94.7 us; the launch traced here: 94.4 us
  Pallas kernels  88.3 us (93%)
  local copies, waits for them, and re-layouts  3.05 us (3%)
  other arithmetic  1.55 us (2%)
  between operations  1.4 us (1%)
    pallas_call x1, Pallas kernels, run_layers(): pl.pallas_call(layer_kernel, out_shape=(jax.ShapeDtypeStruct((rows, share...  88.3 us
    unnamed x6, local copies, waits for them, and re-layouts  2.93 us

profile of v5, /device:TPU:32, one launch (start us, length us, event | category | flops | bytes accessed | tf_op | source)
XLA Modules:
  0.0 94.4 jit_solution(9321393436652216027)
XLA Ops:
  0.6 0.0 copy-start
  1.5 0.1 copy-done
  1.6 0.1 fusion
  1.7 0.1 dynamic_update_slice.3
  1.8 0.0 copy-start.1
  1.8 0.7 convert_element_type.45
  2.5 0.8 multiply_select_fusion
  3.3 0.0 copy-done.1
  3.3 88.3 %shard_map.104 = (bf16[32,768]{1,0:T(8,128)(2,1)}, bf16[2,32,384]{2,1,0:T(8,128)(2,1)}) custom-call(bf16[32,768]{1,0:T(8,128)(2,1)} %hidden_ref.1, bf16[3,3072,384]{2,1,0:T(8,128)(2,1)} %bitcast.21, bf16[384,3072]{1,0:T(8,128)(2,1)} %bitcast.22, bf16[2,32,384]{2,1,0:T(8,128)(2,1)} %bitcast.23, f32[2,128]{1,0:T(2,128)} %bitcast.27, f32[2,64]{1,0:T(2,128)} %bitcast.26, ...), custom_call_target="tpu_custom_call" | custom-call | tf_op jit(solution)/shard_map/pallas_call | solution.py:474
  91.6 1.4 %copy.15 = bf16[1,32,768]{2,1,0:T(8,128)(2,1)} copy(bf16[1,32,768]{2,1,0:T(8,128)(2,1)} %bitcast.25) | data formatting | bytes 98304
  93.0 1.4 %copy.16 = bf16[1,2,32,384]{3,2,1,0:T(8,128)(2,1)} copy(bf16[1,2,32,384]{3,2,1,0:T(8,128)(2,1)} %bitcast.24) | data formatting | bytes 98304
  (8 shorter events, 0.1 us)
Async XLA Ops:
  0.6 0.9 copy-start
  1.8 1.5 %copy-start.1 = (f32[1,256]{1,0:T(1,128)}, f32[1,256]{1,0:T(1,128)S(1)}, u32[]{:S(2)}) copy-start(f32[1,256]{1,0:T(1,128)S(1)} %dynamic_update_slice.3) | copy-start | bytes 3076

commit v6 on v4

--- a/solution.py
+++ b/solution.py
@@ -346,10 +346,6 @@
     value_gather = SeqGather(kv_ref.at[1], fresh_values, value_send, value_recv)
     value_gather.start()
 
-    @pl.when(section == 0)
-    def _():
-        stale.forward_x()
-
     queries = head_norm_rope(project(0), gains[0:1], cosine, sine)
     stacked = jnp.concatenate([queries] * heads, axis=0)
     row_head = lax.broadcasted_iota(jnp.int32, stacked.shape, 0) // rows
@@ -360,6 +356,12 @@
 
     @pl.when(section == 0)
     def _():
+        stale.forward_x()
+
+    key_gather.forward_x()
+
+    @pl.when(section == 0)
+    def _():
         stale.finish()
 
     tokens = rows * 32
@@ -371,7 +373,6 @@
     scores_stale = lax.dot_general(
         spread, all_rows(stale_all[:, :, :, 0]), contract, preferred_element_type=jnp.float32
     )
-    key_gather.forward_x()
     key_gather.finish()
     scores_fresh = lax.dot_general(
         spread, all_rows(fresh_keys[...]), contract, preferred_element_type=jnp.float32
@@ -388,10 +389,10 @@
     denominator = jnp.sum(weights, axis=1, keepdims=True)
     part_fresh = jnp.where(allowed, weights, 0.0).astype(jnp.bfloat16)
     part_stale = jnp.where(allowed, 0.0, weights).astype(jnp.bfloat16)
+    value_gather.forward_x()
     mixed = jnp.dot(
         part_stale, all_rows(stale_all[:, :, :, 1]), preferred_element_type=jnp.float32
     )
-    value_gather.forward_x()
     value_gather.finish()
     mixed += jnp.dot(part_fresh, all_rows(fresh_values[...]), preferred_element_type=jnp.float32)
     mixed = jnp.where(row_head == col_head, mixed / denominator, 0.0)

time: 78.3 us -> 77.9 us (level)
  no operation moved by 1% of the time
where the time goes in v6:
time: 77.9 us; the launch traced here: 77.6 us
  Pallas kernels  71.5 us (92%)
  local copies, waits for them, and re-layouts  3.05 us (4%)
  other arithmetic  1.55 us (2%)
  between operations  1.4 us (2%)
    pallas_call x1, Pallas kernels, run_layers(): pl.pallas_call(layer_kernel, out_shape=(jax.ShapeDtypeStruct((rows, share...  71.5 us
    unnamed x6, local copies, waits for them, and re-layouts  2.93 us

profile of v6, /device:TPU:32, one launch (start us, length us, event | category | flops | bytes accessed | tf_op | source)
XLA Modules:
  0.0 77.6 jit_solution(9610564009793125647)
XLA Ops:
  0.6 0.0 copy-start
  1.5 0.1 copy-done
  1.6 0.1 fusion
  1.7 0.1 dynamic_update_slice.3
  1.8 0.0 copy-start.1
  1.8 0.7 convert_element_type.45
  2.5 0.8 multiply_select_fusion
  3.3 0.0 copy-done.1
  3.3 71.5 %shard_map.104 = (bf16[32,768]{1,0:T(8,128)(2,1)}, bf16[2,32,384]{2,1,0:T(8,128)(2,1)}) custom-call(bf16[32,768]{1,0:T(8,128)(2,1)} %hidden_ref.1, bf16[3,3072,384]{2,1,0:T(8,128)(2,1)} %bitcast.21, bf16[384,3072]{1,0:T(8,128)(2,1)} %bitcast.22, bf16[2,32,384]{2,1,0:T(8,128)(2,1)} %bitcast.23, f32[2,128]{1,0:T(2,128)} %bitcast.27, f32[2,64]{1,0:T(2,128)} %bitcast.26, ...), custom_call_target="tpu_custom_call" | custom-call | tf_op jit(solution)/shard_map/pallas_call | solution.py:459
  74.8 1.4 %copy.15 = bf16[1,32,768]{2,1,0:T(8,128)(2,1)} copy(bf16[1,32,768]{2,1,0:T(8,128)(2,1)} %bitcast.25) | data formatting | bytes 98304
  76.2 1.4 %copy.16 = bf16[1,2,32,384]{3,2,1,0:T(8,128)(2,1)} copy(bf16[1,2,32,384]{3,2,1,0:T(8,128)(2,1)} %bitcast.24) | data formatting | bytes 98304
  (8 shorter events, 0.1 us)
Async XLA Ops:
  0.6 0.9 %copy-start = (bf16[1,512,144]{1,2,0:T(8,128)(2,1)S(1)}, bf16[1,512,144]{1,2,0:T(8,128)(2,1)}, u32[]{:S(2)}) copy-start(bf16[1,512,144]{1,2,0:T(8,128)(2,1)} %param.13) | copy-start | bytes 442372
  1.8 1.5 %copy-start.1 = (f32[1,256]{1,0:T(1,128)}, f32[1,256]{1,0:T(1,128)S(1)}, u32[]{:S(2)}) copy-start(f32[1,256]{1,0:T(1,128)S(1)} %dynamic_update_slice.3) | copy-start | bytes 3076

commit v7 on v6

--- a/solution.py
+++ b/solution.py
@@ -264,6 +264,11 @@
                 column_copy(0, (z + dz) % 4, (c + dc) % 2).wait_recv()
     for k in range(15):
         plane_copy(k, x, tp).start()
+
+    @pl.when(section == 0)
+    def _():
+        stale.forward_z()
+
     for dx in (0,) + OTHERS:
         for dt in (0,) + OTHERS:
             if (dx, dt) != (0, 0):
@@ -277,11 +282,7 @@
     @pl.when(section == 1)
     def _():
         stale.start()
-
-    stale.forward_z()
-
-    @pl.when(section == 1)
-    def _():
+        stale.forward_z()
         stale.forward_x()
         stale.finish()
         x_arrived(tp)

time: 77.9 us -> 76.5 us (0.982)
  Pallas kernels: 71.5 us -> 70.1 us
    pallas_call x1, Pallas kernels: 71.5 us -> 70.1 us  [run_layers(): pl.pallas_call(layer_kernel, out_shape=(jax.ShapeDtypeStruct((rows, share...]
where the time goes in v7:
time: 76.5 us; the launch traced here: 76.2 us
  Pallas kernels  70.1 us (92%)
  local copies, waits for them, and re-layouts  3.05 us (4%)
  other arithmetic  1.55 us (2%)
  between operations  1.4 us (2%)
    pallas_call x1, Pallas kernels, run_layers(): pl.pallas_call(layer_kernel, out_shape=(jax.ShapeDtypeStruct((rows, share...  70.1 us
    unnamed x6, local copies, waits for them, and re-layouts  2.93 us

profile of v7, /device:TPU:32, one launch (start us, length us, event | category | flops | bytes accessed | tf_op | source)
XLA Modules:
  0.0 76.2 jit_solution(908558036964158410)
XLA Ops:
  0.6 0.0 copy-start
  1.5 0.1 copy-done
  1.6 0.1 fusion
  1.7 0.1 dynamic_update_slice.3
  1.8 0.0 copy-start.1
  1.8 0.7 convert_element_type.45
  2.5 0.8 %multiply_select_fusion = (f32[32,128]{1,0:T(8,128)}, f32[32,128]{1,0:T(8,128)}) fusion(f32[128]{0:T(128)S(1)} %get-tuple-element.13, f32[128]{0:T(128)S(1)} %get-tuple-element.14, f32[32]{0:T(128)S(1)} %get-tuple-element.9, f32[128]{0:T(128)S(1)} %get-tuple-element.15, f32[32]{0:T(128)S(1)} %get-tuple-element.10, f32[128]{0:T(128)S(1)} %get-tuple-element.16, ...), kind=kLoop, calls=%fused_computation.2 | loop fusion | flops 32768 | bytes 35232 | tf_op jit(solution)/shard_map/jit(_where)/select_n | solution.py:515
  3.3 0.0 copy-done.1
  3.3 70.1 %shard_map.104 = (bf16[32,768]{1,0:T(8,128)(2,1)}, bf16[2,32,384]{2,1,0:T(8,128)(2,1)}) custom-call(bf16[32,768]{1,0:T(8,128)(2,1)} %hidden_ref.1, bf16[3,3072,384]{2,1,0:T(8,128)(2,1)} %bitcast.21, bf16[384,3072]{1,0:T(8,128)(2,1)} %bitcast.22, bf16[2,32,384]{2,1,0:T(8,128)(2,1)} %bitcast.23, f32[2,128]{1,0:T(2,128)} %bitcast.27, f32[2,64]{1,0:T(2,128)} %bitcast.26, ...), custom_call_target="tpu_custom_call" | custom-call | tf_op jit(solution)/shard_map/pallas_call | solution.py:460
  73.3 1.4 %copy.15 = bf16[1,32,768]{2,1,0:T(8,128)(2,1)} copy(bf16[1,32,768]{2,1,0:T(8,128)(2,1)} %bitcast.25) | data formatting | bytes 98304
  74.8 1.4 %copy.16 = bf16[1,2,32,384]{3,2,1,0:T(8,128)(2,1)} copy(bf16[1,2,32,384]{3,2,1,0:T(8,128)(2,1)} %bitcast.24) | data formatting | bytes 98304
  (8 shorter events, 0.1 us)
Async XLA Ops:
  0.6 0.9 %copy-start = (bf16[1,512,144]{1,2,0:T(8,128)(2,1)S(1)}, bf16[1,512,144]{1,2,0:T(8,128)(2,1)}, u32[]{:S(2)}) copy-start(bf16[1,512,144]{1,2,0:T(8,128)(2,1)} %param.13) | copy-start | bytes 442372
  1.8 1.5 %copy-start.1 = (f32[1,256]{1,0:T(1,128)}, f32[1,256]{1,0:T(1,128)S(1)}, u32[]{:S(2)}) copy-start(f32[1,256]{1,0:T(1,128)S(1)} %dynamic_update_slice.3) | copy-start | bytes 3076
